TPU v7x, 32 devices: a whole 2x2x4 slice. The times are simulated.
32 devices in a mesh: frow: 4 (over x, core), fcol: 8 (over z, y).
Axes of the slice: x: 2, y: 2, z: 4, core: 2. Of those that a mesh axis runs over, the one named last changes fastest.
Arguments:
- facet_image: bfloat16 [2048, 4096], P('frow', 'fcol'), may hold values from -6 to 6
- row_offsets: int32 [2], replicated, may hold values from 0 to 65280
- col_offsets: int32 [2], replicated, may hold values from 0 to 65280
- vis_subgrid: int32 [16384], P(('frow', 'fcol')), may hold values from 0 to 3
- vis_u: int32 [16384], P(('frow', 'fcol')), may hold values from 0 to 255
- vis_v: int32 [16384], P(('frow', 'fcol')), may hold values from 0 to 255
- observed: float32 [2, 16384], P(None, ('frow', 'fcol')), may hold values from -6 to 6
Outputs:
- facet_residual: float32 [2048, 4096], P('frow', 'fcol')
- residual_vis: float32 [2, 16384], P(None, ('frow', 'fcol'))
Inputs may be any that keep to these rules, and one draw needn't show every extreme that they name: `vis_subgrid`: subgrid numbers count row by row over the 2 x 2 subgrids.
All inputs are finite; a program needn't handle non-finite values.
Results may differ from a plain program's by a relative error of at most 0.023.
Values may be sent and summed in bfloat16 or wider, within the bound.
A program may use at most 64 MiB of HBM per device.

v0:
```python
import math

import jax
import jax.numpy as jnp
from jax import lax
from jax.sharding import PartitionSpec as P

SKY = 65536
SG = 256
NR = 2
NC = 2


def wrapped(frequency, position):
    high_part = frequency // 256
    low_part = frequency % 256
    return (high_part * (position * 256 % SKY) + low_part * position) % SKY


def sky_tables(start, positions):
    frequency = start + jnp.arange(SG, dtype=jnp.int32)[:, None]
    angles = wrapped(frequency, positions[None, :]).astype(jnp.float32) * (2.0 * math.pi / SKY)
    return (jnp.cos(angles).astype(jnp.bfloat16), jnp.sin(angles).astype(jnp.bfloat16))


def grid_tables():
    counter = jnp.arange(SG, dtype=jnp.int32)
    angles = (counter[:, None] * counter[None, :] % SG).astype(jnp.float32) * (2.0 * math.pi / SG)
    return (jnp.cos(angles).astype(jnp.bfloat16), jnp.sin(angles).astype(jnp.bfloat16))


def contract_first(left, right):
    return lax.dot_general(
        left, right, (((0,), (0,)), ((), ())), preferred_element_type=jnp.float32
    )


def contract_last(left, right):
    return lax.dot_general(
        left, right, (((1,), (1,)), ((), ())), preferred_element_type=jnp.float32
    )


def shards(facet_image, row_offsets, col_offsets, vis_subgrid, vis_u, vis_v, observed):
    f32 = jnp.float32
    bf16 = jnp.bfloat16
    rows_count = lax.axis_size("frow")
    cols_count = lax.axis_size("fcol")
    facet_side = facet_image.shape[0]
    subgrids = NR * NC
    scale_in = 1.0 / (facet_side * math.sqrt(rows_count * cols_count))
    scale_out = 1.0 / (SG * math.sqrt(subgrids))
    row_pos = lax.axis_index("frow") * (SKY // rows_count) + jnp.arange(
        facet_side, dtype=jnp.int32
    ) * (SKY // (rows_count * facet_side))
    col_pos = lax.axis_index("fcol") * (SKY // cols_count) + jnp.arange(
        facet_side, dtype=jnp.int32
    ) * (SKY // (cols_count * facet_side))
    row_tabs = [
        jnp.concatenate(sky_tables(row_offsets[row_pick], row_pos), 0) for row_pick in range(NR)
    ]
    col_tabs = [
        jnp.concatenate(sky_tables(col_offsets[col_pick], col_pos), 0) for col_pick in range(NC)
    ]
    col_halves = [
        contract_last(facet_image, col_tabs[col_pick]).astype(bf16) for col_pick in range(NC)
    ]
    blocks_out = []
    for row_pick in range(NR):
        for col_pick in range(NC):
            product = jnp.dot(row_tabs[row_pick], col_halves[col_pick], preferred_element_type=f32)
            part_real = product[:SG, :SG] - product[SG:, SG:]
            part_imag = -(product[:SG, SG:] + product[SG:, :SG])
            blocks_out.append(jnp.concatenate([part_real, part_imag], 1) * scale_in)
    stacked = jnp.concatenate(blocks_out, 0)
    summed = lax.psum(stacked, ("frow", "fcol"))
    grid_bf = summed.astype(bf16)
    kcos, ksin = grid_tables()
    forward_block = jnp.concatenate(
        [jnp.concatenate([kcos, ksin], 1), jnp.concatenate([-ksin, kcos], 1)], 0
    )
    w_both = (
        jnp.dot(grid_bf, forward_block, preferred_element_type=f32)
        .astype(bf16)
        .reshape(subgrids, SG, 2 * SG)
    )
    with_cos = jnp.einsum("au,sav->suv", kcos, w_both, preferred_element_type=f32)
    with_sin = jnp.einsum("au,sav->suv", ksin, w_both, preferred_element_type=f32)
    hat_real = (with_cos[:, :, :SG] - with_sin[:, :, SG:]) / SG
    hat_imag = (with_sin[:, :, :SG] + with_cos[:, :, SG:]) / SG
    cell_ids = (vis_subgrid * SG + vis_u) * SG + vis_v
    model_vis = jnp.stack(
        [jnp.take(hat_real.reshape(-1), cell_ids), jnp.take(hat_imag.reshape(-1), cell_ids)]
    )
    residual = observed - model_vis
    cells_all = subgrids * SG * SG
    inverse_block = jnp.concatenate(
        [jnp.concatenate([kcos, -ksin], 1), jnp.concatenate([ksin, kcos], 1)], 0
    )
    local_real = jax.ops.segment_sum(residual[0], cell_ids, num_segments=cells_all)
    local_imag = jax.ops.segment_sum(residual[1], cell_ids, num_segments=cells_all)
    ghat_real, ghat_imag = lax.psum((local_real, local_imag), ("frow", "fcol"))
    ghat_both = jnp.concatenate(
        [
            ghat_real.reshape(subgrids * SG, SG).astype(bf16),
            ghat_imag.reshape(subgrids * SG, SG).astype(bf16),
        ],
        1,
    )
    v_flat = jnp.dot(ghat_both, inverse_block, preferred_element_type=f32).astype(bf16)
    v_both = v_flat.reshape(subgrids, SG, 2 * SG)
    back_cos = jnp.einsum("au,suv->sav", kcos, v_both, preferred_element_type=f32)
    back_sin = jnp.einsum("au,suv->sav", ksin, v_both, preferred_element_type=f32)
    back_real = ((back_cos[:, :, :SG] + back_sin[:, :, SG:]) / SG).astype(bf16)
    back_imag = ((back_cos[:, :, SG:] - back_sin[:, :, :SG]) / SG).astype(bf16)
    image = jnp.zeros((facet_side, facet_side), f32)
    for col_pick in range(NC):
        u_both = jnp.zeros((facet_side, 2 * SG), f32)
        for row_pick in range(NR):
            sub_index = row_pick * NC + col_pick
            g_real = back_real[sub_index]
            g_imag = back_imag[sub_index]
            right_side = jnp.concatenate(
                [jnp.concatenate([g_real, g_imag], 1), jnp.concatenate([-g_imag, g_real], 1)], 0
            )
            u_both = u_both + contract_first(row_tabs[row_pick], right_side)
        col_cos = col_tabs[col_pick][:SG]
        col_sin = col_tabs[col_pick][SG:]
        image = image + jnp.dot(
            u_both.astype(bf16), jnp.concatenate([col_cos, -col_sin], 0), preferred_element_type=f32
        )
    return (image * scale_out, residual)


def solution(mesh):
    in_specs = (
        P("frow", "fcol"),
        P(),
        P(),
        P(("frow", "fcol")),
        P(("frow", "fcol")),
        P(("frow", "fcol")),
        P(None, ("frow", "fcol")),
    )
    out_specs = (P("frow", "fcol"), P(None, ("frow", "fcol")))
    return jax.shard_map(shards, mesh=mesh, in_specs=in_specs, out_specs=out_specs, check_vma=False)
```

profile of v0, /device:TPU:0, one launch (start us, length us, event | category | flops | bytes accessed | tf_op | source)
XLA Modules:
  0.0 194.2 jit_solution(18069458550596602750)
XLA Ops:
  0.7 1.3 fusion.145
  2.0 0.7 and_select_fusion.4
  2.7 0.7 and_select_fusion.2
  3.3 4.6 %sine_convert_fusion.2 = (bf16[256,512]{1,0:T(8,128)(2,1)S(1)}, bf16[256,512]{1,0:T(8,128)(2,1)S(1)}, bf16[256,512]{1,0:T(8,128)(2,1)S(1)}, bf16[256,512]{1,0:T(8,128)(2,1)S(1)}) fusion(s32[512]{0:T(512)S(1)} %get-tuple-element.54, s32[256]{0:T(256)S(1)} %get-tuple-element.55, s32[512]{0:T(512)S(1)} %get-tuple-element.53, s32[256]{0:T(256)S(1)} %get-tuple-element.56, ...), kind=kLoop, calls=%fused_computation.116 | loop fusion | flops 4718592 | bytes 1056768 | tf_op jit(solution)/shard_map/convert_element_type | solution.py:23
  8.0 0.7 copy-done.5
  8.7 0.5 convolution_convert_fusion.3
  9.2 0.6 fusion.144
  9.8 0.7 and_select_fusion.6
  10.4 0.7 and_select_fusion
  11.1 4.6 %cosine_convert_fusion.3 = (bf16[256,512]{1,0:T(8,128)(2,1)S(1)}, bf16[256,512]{1,0:T(8,128)(2,1)S(1)}, bf16[256,512]{1,0:T(8,128)(2,1)S(1)}, bf16[256,512]{1,0:T(8,128)(2,1)S(1)}) fusion(s32[512]{0:T(512)S(1)} %get-tuple-element.60, s32[256]{0:T(256)S(1)} %get-tuple-element.61, s32[512]{0:T(512)S(1)} %get-tuple-element.59, s32[256]{0:T(256)S(1)} %get-tuple-element.62, ...), kind=kLoop, calls=%fused_computation.123 | loop fusion | flops 4718592 | bytes 1056768 | tf_op jit(solution)/shard_map/convert_element_type | solution.py:23
  15.8 0.5 fusion.142
  16.4 0.5 convolution_convert_fusion.2
  16.9 0.5 fusion.141
  17.5 0.5 fusion.140
  18.0 0.1 slice_subtract_fusion.3
  18.1 0.5 fusion.139
  18.7 0.2 pad_maximum_fusion
  19.0 64.4 %all-reduce.3 = bf16[1024,512]{0,1:T(8,128)(2,1)} all-reduce(f32[1024,512]{0,1:T(8,128)S(1)} %pad_maximum_fusion), channel_id=1, replica_groups=mesh['frow'=4,'fcol'=8] {'frow','fcol'}, use_global_device_ids=true, to_apply=%region_0.1 | all-reduce | flops 524288 | bytes 3145728 | tf_op jit(solution)/shard_map/psum | solution.py:76
  83.4 1.1 sine_convert_fusion.4
  84.5 1.0 fusion.100
  85.5 2.0 %convolution_convert_fusion.1 = bf16[1024,512]{1,0:T(8,128)(2,1)S(1)} fusion(bf16[1024,512]{0,1:T(8,128)(2,1)} %all-reduce.3, bf16[256,256]{1,0:T(8,128)(2,1)S(1)} %get-tuple-element.66, bf16[256,256]{1,0:T(8,128)(2,1)S(1)} %fusion.100, bf16[256,256]{1,0:T(8,128)(2,1)S(1)} %get-tuple-element.65), kind=kOutput, calls=%fused_computation.10 | convolution fusion | flops 539492352 | bytes 2490368 | tf_op jit(solution)/shard_map/dot_general | solution.py:83
  87.5 1.4 convolution_bitcast_fusion.2
  88.9 1.4 convolution_bitcast_fusion.3
  90.3 1.3 fusion.9
  91.6 0.3 copy.16
  92.0 0.5 copy.24
  92.5 0.1 copy-done.22
  92.7 0.6 compare_select_fusion
  93.3 4.3 %gather_fusion.1 = f32[512]{0:T(512)} fusion(f32[262144]{0:T(1024)S(1)} %bitcast.67, s32[1024]{0:T(1024)S(1)} %pad_clamp_fusion), kind=kCustom, calls=%fused_computation.1.clone | custom fusion | bytes 6144 | tf_op jit(solution)/shard_map/jit(_take)/gather | solution.py:93
  97.5 1.6 copy.15
  99.1 0.5 copy.23
  99.7 3.1 %gather_fusion = f32[512]{0:T(512)S(1)} fusion(f32[262144]{0:T(1024)S(1)} %bitcast.68, s32[1024]{0:T(1024)S(1)} %pad_clamp_fusion), kind=kCustom, calls=%fused_computation.clone | custom fusion | bytes 6144 | tf_op jit(solution)/shard_map/jit(_take)/gather | solution.py:93
  102.9 0.6 fusion.143
  103.5 3.5 %scatter_custom_fusion = f32[262144]{0:T(1024)S(1)} fusion(s32[512]{0:T(512)S(1)} %copy-done.18, f32[512]{0:T(512)S(1)} %bitcast.78, f32[]{:T(128)} %constant.156.clone.1), kind=kCustom, calls=%fused_computation.120 | custom fusion | flops 512 | bytes 1048580 | tf_op jit(solution)/shard_map/scatter-add | solution.py:100
  107.0 3.7 %scatter_custom_fusion.1 = f32[262144]{0:T(1024)S(1)} fusion(s32[512]{0:T(512)} %get-tuple-element.6, f32[512]{0:T(512)} %bitcast.77, f32[]{:T(128)} %constant.156.clone.1), kind=kCustom, calls=%fused_computation.118 | custom fusion | flops 512 | bytes 1049088 | tf_op jit(solution)/shard_map/scatter-add | solution.py:101
  110.7 62.5 %all-reduce.4 = (bf16[262144]{0:T(1024)(128)(2,1)}, bf16[262144]{0:T(1024)(128)(2,1)}) all-reduce(f32[262144]{0:T(1024)S(1)} %scatter_custom_fusion.1, f32[262144]{0:T(1024)S(1)} %scatter_custom_fusion), channel_id=1, replica_groups=mesh['frow'=4,'fcol'=8] {'frow','fcol'}, use_global_device_ids=true, to_apply=%region_4.6 | all-reduce | flops 524288 | bytes 3145728 | tf_op jit(solution)/shard_map/psum | solution.py:102
  173.2 1.3 convert_element_type.148
  174.4 1.2 convert_element_type.150
  175.7 0.7 convolution_convert_fusion
  176.4 1.4 convolution_bitcast_fusion
  177.8 1.4 convolution_bitcast_fusion.1
  179.2 0.4 fusion.5
  179.7 0.8 copy-done.2
  180.6 1.5 fusion.59
  182.0 1.5 fusion.36
  183.5 4.4 %fusion.138 = (bf16[256,512]{1,0:T(8,128)(2,1)S(1)}, bf16[256,512]{1,0:T(8,128)(2,1)S(1)}) fusion(s32[512]{0:T(512)S(1)} %get-tuple-element.54, s32[256]{0:T(256)S(1)} %copy-done.15, s32[512]{0:T(512)S(1)} %get-tuple-element.53, s32[256]{0:T(256)S(1)} %copy-done.17, s32[256]{0:T(256)S(1)} %get-tuple-element.55, s32[256]{0:T(256)S(1)} %copy-done.13), kind=kLoop, calls=%fused_computation.238 | loop fusion | flops 5242880 | bytes 532480 | tf_op jit(solution)/shard_map/neg | solution.py:130
  187.9 3.0 %fusion.3 = f32[512,512]{1,0:T(8,128)} fusion(f32[512,512]{1,0:T(8,128)} %fusion.36, bf16[256,512]{1,0:T(8,128)(2,1)S(1)} %copy-done.6, bf16[256,256]{0,1:T(8,128)(2,1)S(1)} %get-tuple-element.29, bf16[256,256]{0,1:T(8,128)(2,1)S(1)} %get-tuple-element.25, bf16[256,256]{0,1:T(8,128)(2,1)S(1)} %get-tuple-element.21, ...), kind=kOutput, calls=%fused_computation.19 | convolution fusion | flops 541589504 | bytes 3538944 | tf_op jit(solution)/shard_map/dot_general | solution.py:129
  190.9 3.3 %fusion = f32[512,512]{1,0:T(8,128)} fusion(f32[512,512]{1,0:T(8,128)} %fusion.3, f32[512,512]{1,0:T(8,128)} %fusion.59, bf16[256,512]{1,0:T(8,128)(2,1)S(1)} %copy-done.4, bf16[256,256]{0,1:T(8,128)(2,1)S(1)} %get-tuple-element.27, bf16[256,256]{0,1:T(8,128)(2,1)S(1)} %get-tuple-element.23, bf16[256,256]{0,1:T(8,128)(2,1)S(1)} %get-tuple-element.19, ...), kind=kOutput, calls=%fused_computation.12 | convolution fusion | flops 542113792 | bytes 4587520 | tf_op jit(solution)/shard_map/dot_general | solution.py:129
  (62 shorter events, 0.7 us)
Async XLA Ops:
  0.6 8.1 %copy-start = (bf16[512,512]{1,0:T(8,128)(2,1)S(1)}, bf16[512,512]{1,0:T(8,128)(2,1)}, u32[]{:S(2)}) copy-start(bf16[512,512]{1,0:T(8,128)(2,1)} %param.9) | copy-start | bytes 1572868
  0.6 8.5 %copy-start.24 = (s32[2]{0:T(128)S(1)}, s32[2]{0:T(128)}, u32[]{:S(2)}) copy-start(s32[2]{0:T(128)} %param.10) | copy-start | bytes 28
  2.7 13.6 %copy-start.12 = (s32[256]{0:T(256)}, s32[256]{0:T(256)S(1)}, u32[]{:S(2)}) copy-start(s32[256]{0:T(256)S(1)} %get-tuple-element.56) | copy-start | bytes 3076
  3.3 12.9 %copy-start.14 = (s32[256]{0:T(256)}, s32[256]{0:T(256)S(1)}, u32[]{:S(2)}) copy-start(s32[256]{0:T(256)S(1)} %get-tuple-element.57) | copy-start | bytes 3076
  3.3 12.9 %copy-start.16 = (s32[256]{0:T(256)}, s32[256]{0:T(256)S(1)}, u32[]{:S(2)}) copy-start(s32[256]{0:T(256)S(1)} %get-tuple-element.58) | copy-start | bytes 3076
  8.0 0.7 copy-start.5
  8.0 8.4 %copy-start.3 = (bf16[256,512]{1,0:T(8,128)(2,1)}, bf16[256,512]{1,0:T(8,128)(2,1)S(1)}, u32[]{:S(2)}) copy-start(bf16[256,512]{1,0:T(8,128)(2,1)S(1)} %get-tuple-element.45) | copy-start | bytes 786436
  15.7 1.1 copy-start.1
  84.5 3.0 %copy-start.7 = (bf16[256,256]{1,0:T(8,128)(2,1)}, bf16[256,256]{1,0:T(8,128)(2,1)S(1)}, u32[]{:S(2)}) copy-start(bf16[256,256]{1,0:T(8,128)(2,1)S(1)} %get-tuple-element.66) | copy-start | bytes 393220
  85.5 2.0 %copy-start.9 = (bf16[256,256]{1,0:T(8,128)(2,1)}, bf16[256,256]{1,0:T(8,128)(2,1)S(1)}, u32[]{:S(2)}) copy-start(bf16[256,256]{1,0:T(8,128)(2,1)S(1)} %fusion.100) | copy-start | bytes 393220
  91.6 0.9 copy-start.21
  92.0 0.7 copy-start.22
  92.0 0.7 copy-start.23
  99.6 3.2 %copy-start.18 = (s32[512]{0:T(512)S(1)}, s32[512]{0:T(512)}, u32[]{:S(2)}) copy-start(s32[512]{0:T(512)} %get-tuple-element.6) | copy-start | bytes 6148
  99.6 3.2 %copy-start.19 = (f32[512]{0:T(512)S(1)}, f32[512]{0:T(512)}, u32[]{:S(2)}) copy-start(f32[512]{0:T(512)} %gather_fusion.1) | copy-start | bytes 6148
  99.7 3.2 %copy-start.20 = (f32[2,512]{1,0:T(2,128)S(1)}, f32[2,512]{1,0:T(2,128)}, u32[]{:S(2)}) copy-start(f32[2,512]{1,0:T(2,128)} %param.15) | copy-start | bytes 12292
  102.9 70.3 %copy-start.11 = (f32[2,512]{1,0:T(2,128)}, f32[2,512]{1,0:T(2,128)S(1)}, u32[]{:S(2)}) copy-start(f32[2,512]{1,0:T(2,128)S(1)} %maximum_subtract_fusion) | copy-start | bytes 12292
  173.2 2.5 %copy-start.8 = (bf16[256,256]{1,0:T(8,128)(2,1)S(1)}, bf16[256,256]{1,0:T(8,128)(2,1)}, u32[]{:S(2)}) copy-start(bf16[256,256]{1,0:T(8,128)(2,1)} %copy-done.7) | copy-start | bytes 393220
  173.2 2.5 %copy-start.10 = (bf16[256,256]{1,0:T(8,128)(2,1)S(1)}, bf16[256,256]{1,0:T(8,128)(2,1)}, u32[]{:S(2)}) copy-start(bf16[256,256]{1,0:T(8,128)(2,1)} %copy-done.9) | copy-start | bytes 393220
  179.6 1.0 copy-start.2
  182.0 1.5 copy-start.13
  182.0 1.5 copy-start.15
  182.0 1.5 copy-start.17
  182.0 5.8 %copy-start.6 = (bf16[256,512]{1,0:T(8,128)(2,1)S(1)}, bf16[256,512]{1,0:T(8,128)(2,1)}, u32[]{:S(2)}) copy-start(bf16[256,512]{1,0:T(8,128)(2,1)} %copy-done.5) | copy-start | bytes 786436
  187.9 3.0 %copy-start.4 = (bf16[256,512]{1,0:T(8,128)(2,1)S(1)}, bf16[256,512]{1,0:T(8,128)(2,1)}, u32[]{:S(2)}) copy-start(bf16[256,512]{1,0:T(8,128)(2,1)} %copy-done.3) | copy-start | bytes 786436
where the time goes:
time: 195 us; the launch traced here: 194 us
  blocking collectives  127 us (65%)
  other arithmetic  28.6 us (15%)
  matrix products  20.3 us (10%)
  local copies, waits for them, and re-layouts  17.1 us (9%)
    psum x1, blocking collectives, shards(): summed = lax.psum(stacked, ('frow', 'fcol'))  64.4 us
    psum x1, blocking collectives, shards(): ghat_real, ghat_imag = lax.psum((local_real, local_imag), ('frow', 'fcol'))  62.5 us
    dot_general x2, matrix products, shards(): jnp.dot(u_both.astype(bf16), jnp.concatenate([col_cos, -col_sin], 0), pre...  6.29 us
    convert_element_type x1, other arithmetic, sky_tables(): jnp.sin(angles).astype(jnp.bfloat16)  4.64 us
    convert_element_type x1, other arithmetic, sky_tables(): jnp.cos(angles).astype(jnp.bfloat16)  4.64 us
    neg x1, other arithmetic, shards(): -col_sin  4.36 us
    gather x1, local copies, waits for them, and re-layouts, shards(): jnp.take(hat_imag.reshape(-1), cell_ids)  4.27 us

commit v1 on v0

v1 whole, which is shorter than its diff:
```python
import functools
import math

import jax
import jax.numpy as jnp
from jax import lax
from jax.experimental import pallas as pl
from jax.experimental.pallas import tpu as pltpu
from jax.sharding import PartitionSpec as P

SKY = 65536
SG = 256
NR = 2
NC = 2
f32 = jnp.float32
bf16 = jnp.bfloat16
i32 = jnp.int32
MESH = pl.DeviceIdType.MESH
VM = pl.BlockSpec(memory_space=pltpu.VMEM)
SM = pl.BlockSpec(memory_space=pltpu.SMEM)
LIMIT = 60 << 20


def geometry():
    rows = lax.axis_size("frow")
    cols = lax.axis_size("fcol")
    nx = rows // 2
    ny = 1 << ((cols.bit_length() - 1) // 2)
    nz = cols // ny
    return rows, cols, nx, ny, nz


def position():
    _, _, _, ny, _ = geometry()
    frow = lax.axis_index("frow")
    fcol = lax.axis_index("fcol")
    return frow // 2, frow % 2, fcol % ny, fcol // ny


def dims(contract):
    return ((contract, contract), ((), ()))


def phase(product):
    angle = (product & (SKY - 1)).astype(f32) * (2.0 * math.pi / SKY)
    return jnp.cos(angle), jnp.sin(angle)


def expand(first, places, c_ref, s_ref):
    n = places.shape[1]
    steps = lax.broadcasted_iota(i32, (16, n), 0)
    c0, s0 = phase(steps * places)
    c1, s1 = phase((first + 16 * steps) * places)
    for k in range(SG // 16):
        ck = c1[k : k + 1]
        sk = s1[k : k + 1]
        c_ref[k * 16 : k * 16 + 16, :] = (ck * c0 - sk * s0).astype(bf16)
        s_ref[k * 16 : k * 16 + 16, :] = (sk * c0 + ck * s0).astype(bf16)


def tables_kernel(fs, ro_ref, co_ref, ar_ref, ai_ref, bt_ref, kk, ks, rc, rs):
    rows, cols, _, _, _ = geometry()
    x, h, _, _ = position()
    expand(0, lax.broadcasted_iota(i32, (1, SG), 1) * (SKY // SG), kk, ks)
    kcos = kk[...]
    ksin = ks[...]

    def compose(n):
        c = rc[:, :n]
        s = rs[:, :n]
        re = jnp.dot(kcos, c, preferred_element_type=f32) + jnp.dot(ksin, s, preferred_element_type=f32)
        im = jnp.dot(ksin, c, preferred_element_type=f32) - jnp.dot(kcos, s, preferred_element_type=f32)
        return re.astype(bf16), im.astype(bf16)

    step = SKY // (cols * fs)
    fcol = lax.axis_index("fcol")
    places = (fcol * fs + lax.broadcasted_iota(i32, (1, fs), 1)) * step
    expand(co_ref[h], places, rc.at[:, :fs], rs.at[:, :fs])
    re, im = compose(fs)
    bt_ref[:SG] = re
    bt_ref[SG:] = im
    step = SKY // (rows * fs)
    places = (x * (2 * fs) + lax.broadcasted_iota(i32, (1, 2 * fs), 1)) * step
    for r in range(NR):
        expand(ro_ref[r], places, rc, rs)
        re, im = compose(2 * fs)
        ar_ref[r * SG : r * SG + SG] = re
        ai_ref[r * SG : r * SG + SG] = im


def tables(fs, ro, co):
    return pl.pallas_call(
        functools.partial(tables_kernel, fs),
        out_shape=[
            jax.ShapeDtypeStruct((NR * SG, 2 * fs), bf16),
            jax.ShapeDtypeStruct((NR * SG, 2 * fs), bf16),
            jax.ShapeDtypeStruct((2 * SG, fs), bf16),
        ],
        in_specs=[SM, SM],
        out_specs=[VM, VM, VM],
        scratch_shapes=[
            pltpu.VMEM((SG, SG), bf16),
            pltpu.VMEM((SG, SG), bf16),
            pltpu.VMEM((SG, 2 * fs), bf16),
            pltpu.VMEM((SG, 2 * fs), bf16),
        ],
        compiler_params=pltpu.CompilerParams(vmem_limit_bytes=LIMIT),
        name="tables",
    )(ro, co)


def everyone(n, cols, me, act):
    def step(d, carry):
        to = lax.rem(me + d, n)
        frm = lax.rem(me - d + n, n)
        act(d, to, frm)
        return carry

    lax.fori_loop(1, n, step, 0)


def greet_all(n, cols, me):
    barrier = pltpu.get_barrier_semaphore()

    def hello(d, to, frm):
        pl.semaphore_signal(barrier, inc=1, device_id=(to // cols, to % cols), device_id_type=MESH)

    everyone(n, cols, me, hello)
    pl.semaphore_wait(barrier, n - 1)


def swap_kernel(facet_ref, vis_ref, pair_ref, all_ref, lsem, ssem, rsem, vs, vr):
    rows, cols, _, _, _ = geometry()
    frow = lax.axis_index("frow")
    fcol = lax.axis_index("fcol")
    h = frow % 2
    n = rows * cols
    me = frow * cols + fcol
    greet_all(n, cols, me)
    sib = frow + 1 - 2 * h
    big = pltpu.make_async_remote_copy(
        facet_ref, pair_ref.at[h], ssem, rsem, device_id=(sib, fcol), device_id_type=MESH
    )
    big.start()

    def link(d, to, slot):
        return pltpu.make_async_remote_copy(
            vis_ref, all_ref.at[slot], vs.at[d], vr.at[d],
            device_id=(to // cols, to % cols), device_id_type=MESH,
        )

    everyone(n, cols, me, lambda d, to, frm: link(d, to, me).start())
    own = pltpu.make_async_copy(facet_ref, pair_ref.at[h], lsem.at[0])
    own.start()
    mine = pltpu.make_async_copy(vis_ref, all_ref.at[me], lsem.at[1])
    mine.start()
    own.wait()
    mine.wait()
    everyone(n, cols, me, lambda d, to, frm: link(d, to, me).wait_send())
    everyone(n, cols, me, lambda d, to, frm: link(d, to, frm).wait_recv())
    big.wait_send()
    pltpu.make_async_remote_copy(
        facet_ref, pair_ref.at[1 - h], ssem, rsem, device_id=(sib, fcol), device_id_type=MESH
    ).wait_recv()


def swap(facet, vis):
    rows, cols, _, _, _ = geometry()
    n = rows * cols
    return pl.pallas_call(
        swap_kernel,
        out_shape=[
            jax.ShapeDtypeStruct((2,) + facet.shape, facet.dtype),
            jax.ShapeDtypeStruct((n,) + vis.shape, vis.dtype),
        ],
        in_specs=[VM, VM],
        out_specs=[VM, VM],
        scratch_shapes=[
            pltpu.SemaphoreType.DMA((2,)),
            pltpu.SemaphoreType.DMA,
            pltpu.SemaphoreType.DMA,
            pltpu.SemaphoreType.DMA((n,)),
            pltpu.SemaphoreType.DMA((n,)),
        ],
        compiler_params=pltpu.CompilerParams(
            collective_id=0, has_side_effects=True, vmem_limit_bytes=LIMIT
        ),
        name="swap",
    )(facet, vis)


def forward_kernel(nx, ny, pair_ref, ar_ref, ai_ref, bt_ref, z_ref, zb_ref):
    fs = pair_ref.shape[1]
    stack = pair_ref[...].reshape(2 * fs, fs)
    p = lax.dot_general(stack, bt_ref[...], (((1,), (1,)), ((), ())), preferred_element_type=f32).astype(bf16)
    part = NR * SG // (nx * ny)
    for b in range(nx * ny):
        cut = slice(b * part, b * part + part)
        one = jnp.dot(ar_ref[cut], p, preferred_element_type=f32)
        two = jnp.dot(ai_ref[cut], p, preferred_element_type=f32)
        zr = one[:, :SG] - two[:, SG:]
        zi = one[:, SG:] + two[:, :SG]
        bx, by = b // ny, b % ny
        z_ref[0, bx, by] = zr
        z_ref[1, bx, by] = zi
        zb_ref[0, bx, by] = zr.astype(bf16)
        zb_ref[1, bx, by] = zi.astype(bf16)


def forward(pair, ar, ai, bt):
    _, _, nx, ny, _ = geometry()
    shape = (2, nx, ny, NR * SG // (nx * ny), SG)
    return pl.pallas_call(
        functools.partial(forward_kernel, nx, ny),
        out_shape=[jax.ShapeDtypeStruct(shape, f32), jax.ShapeDtypeStruct(shape, bf16)],
        in_specs=[VM] * 4,
        out_specs=[VM] * 2,
        compiler_params=pltpu.CompilerParams(vmem_limit_bytes=LIMIT),
        name="forward",
    )(pair, ar, ai, bt)


def decode(vis, rows_own):
    _, _, nx, ny, nz = geometry()
    x, h, y, z = position()
    base = ((x * ny + y) * nz + z) * rows_own
    cell = vis[0:1].astype(i32)
    sub = cell // (SG * SG)
    row = (sub // NC) * SG + (cell // SG) % SG - base
    row = jnp.where(sub % NC == h, row, -1)
    n = vis.shape[1]
    hot_row = lax.broadcasted_iota(i32, (rows_own, n), 0) == row
    hot_col = lax.broadcasted_iota(i32, (SG, n), 0) == cell % SG
    return hot_row, jnp.where(hot_col, 1.0, 0.0).astype(bf16)


def grid_kernel(rows_own, all_ref, o_ref, n_ref, acc):
    count = all_ref.shape[0]
    acc[...] = jnp.zeros_like(acc)

    def step(k, carry):
        vis = all_ref[k]
        hot_row, hot_col = decode(vis, rows_own)
        parts = []
        for q in (1, 2):
            val = vis[q : q + 1]
            high = val.astype(bf16).astype(f32)
            parts += [high, val - high]
        parts.append(jnp.ones_like(vis[0:1]))
        left = jnp.concatenate([jnp.where(hot_row, v, 0.0) for v in parts], 0).astype(bf16)
        acc[...] += lax.dot_general(left, hot_col, (((1,), (1,)), ((), ())), preferred_element_type=f32)
        return carry

    lax.fori_loop(0, count, step, 0)
    got = [acc[q * rows_own : (q + 1) * rows_own] for q in range(5)]
    o_ref[:, :SG] = got[0] + got[1]
    o_ref[:, SG:] = got[2] + got[3]
    n_ref[:, :SG] = got[4]
    n_ref[:, SG:] = got[4]


def gridding(vis_all, rows_own):
    shape = jax.ShapeDtypeStruct((rows_own, 2 * SG), f32)
    return pl.pallas_call(
        functools.partial(grid_kernel, rows_own),
        out_shape=[shape, shape],
        in_specs=[VM],
        out_specs=[VM, VM],
        scratch_shapes=[pltpu.VMEM((5 * rows_own, SG), f32)],
        compiler_params=pltpu.CompilerParams(vmem_limit_bytes=LIMIT),
        name="gridding",
    )(vis_all)


def degrid_kernel(rows_own, m_ref, all_ref, out_ref):
    count = all_ref.shape[0]
    m = m_ref[...]
    both = jnp.concatenate([m[:, :SG], m[:, SG:]], 0)
    high = both.astype(bf16)
    low = (both - high.astype(f32)).astype(bf16)

    def step(k, carry):
        hot_row, hot_col = decode(all_ref[k], rows_own)
        val = jnp.dot(high, hot_col, preferred_element_type=f32) + jnp.dot(low, hot_col, preferred_element_type=f32)
        re = jnp.sum(jnp.where(hot_row, val[:rows_own], 0.0), 0, keepdims=True)
        im = jnp.sum(jnp.where(hot_row, val[rows_own:], 0.0), 0, keepdims=True)
        out_ref[k] = jnp.concatenate([re, im], 0)
        return carry

    lax.fori_loop(0, count, step, 0)


def degrid(m, vis_all):
    count, _, nv = vis_all.shape
    return pl.pallas_call(
        functools.partial(degrid_kernel, m.shape[0]),
        out_shape=jax.ShapeDtypeStruct((count, 2, nv), f32),
        in_specs=[VM, VM],
        out_specs=VM,
        compiler_params=pltpu.CompilerParams(vmem_limit_bytes=LIMIT),
        name="degrid",
    )(m, vis_all)


def reduce_kernel(
    scale, z_ref, zb_ref, o_ref, n_ref, m_ref, g_ref,
    acc_a, acc_b, send_a, send_b, got_a1, got_b1, got_a2, got_b2,
    own_z, send_z, got_z, gz, ssem, rsem,
):
    _, _, nx, ny, nz = geometry()
    x, h, y, z = position()
    rows_own = m_ref.shape[0]

    def peer(dx, dy, dz):
        px = lax.rem(x + dx + nx, nx)
        py = lax.rem(y + dy + ny, ny)
        pz = lax.rem(z + dz + nz, nz)
        return (px * 2 + h, pz * ny + py), px, py, pz

    barrier = pltpu.get_barrier_semaphore()
    friends = (
        [(d, 0, 0) for d in range(1, nx)] + [(0, d, 0) for d in range(1, ny)] + [(0, 0, d) for d in range(1, nz)]
    )
    for dx, dy, dz in friends:
        pl.semaphore_signal(barrier, inc=1, device_id=peer(dx, dy, dz)[0], device_id_type=MESH)
    pl.semaphore_wait(barrier, len(friends))
    used = [0]

    def send(src, dst, to):
        k = used[0]
        used[0] += 1
        copy = pltpu.make_async_remote_copy(
            src, dst, ssem.at[k], rsem.at[k], device_id=to, device_id_type=MESH
        )
        copy.start()
        return copy, k

    def land(copies, dst=None):
        for t, (copy, k) in enumerate(copies):
            copy.wait_send()
            if dst is None:
                copy.wait_recv()
            else:
                pltpu.make_async_remote_copy(
                    dst[t], dst[t], ssem.at[k], rsem.at[k], device_id=peer(0, 0, 0)[0], device_id_type=MESH
                ).wait_recv()

    first_a, first_b = [], []
    for d in range(1, nx):
        to, px, _, _ = peer(d, 0, 0)
        first_a.append(send(zb_ref.at[0, px], got_a1.at[d - 1], to))
    for d in range(1, ny):
        to, _, py, _ = peer(0, d, 0)
        first_b.append(send(zb_ref.at[1, :, py], got_b1.at[d - 1], to))
    land(first_a)
    total = z_ref[0, x]
    for d in range(nx - 1):
        total = total + got_a1[d].astype(f32)
    acc_a[...] = total
    send_a[...] = total.astype(bf16)
    second_a, second_b = [], []
    for d in range(1, ny):
        to, _, py, _ = peer(0, d, 0)
        second_a.append(send(send_a.at[py], got_a2.at[d - 1], to))
    land(first_b)
    total = z_ref[1, :, y]
    for d in range(ny - 1):
        total = total + got_b1[d].astype(f32)
    acc_b[...] = total
    send_b[...] = total.astype(bf16)
    for d in range(1, nx):
        to, px, _, _ = peer(d, 0, 0)
        second_b.append(send(send_b.at[px], got_b2.at[d - 1], to))
    land(second_a)
    re = acc_a[y]
    for d in range(ny - 1):
        re = re + got_a2[d].astype(f32)
    land(second_b)
    im = acc_b[x]
    for d in range(nx - 1):
        im = im + got_b2[d].astype(f32)
    for k in range(nz):
        cut = slice(k * rows_own, (k + 1) * rows_own)
        own_z[k, :, :SG] = re[cut]
        own_z[k, :, SG:] = im[cut]
        send_z[k, :, :SG] = re[cut].astype(bf16)
        send_z[k, :, SG:] = im[cut].astype(bf16)
    third = []
    for d in range(1, nz):
        to, _, _, pz = peer(0, 0, d)
        third.append(send(send_z.at[pz], got_z.at[d - 1], to))
    land(third)
    total = own_z[z]
    for d in range(nz - 1):
        total = total + got_z[d].astype(f32)
    model = total * scale
    m_ref[...] = model
    gz[z] = (o_ref[...] - n_ref[...] * model).astype(bf16)
    fourth, dst = [], []
    for d in range(1, nz):
        to, _, _, _ = peer(0, 0, d)
        fourth.append(send(gz.at[z], gz.at[z], to))
        dst.append(gz.at[peer(0, 0, -d)[3]])
    land(fourth, dst)
    for k in range(nz):
        cut = slice(k * rows_own, (k + 1) * rows_own)
        g_ref[0, x, y, cut, :] = gz[k, :, :SG]
        g_ref[1, x, y, cut, :] = gz[k, :, SG:]
    fifth_a, fifth_b, dst_a, dst_b = [], [], [], []
    for d in range(1, ny):
        fifth_a.append(send(g_ref.at[0, x, y], g_ref.at[0, x, y], peer(0, d, 0)[0]))
        dst_a.append(g_ref.at[0, x, peer(0, -d, 0)[2]])
    for d in range(1, nx):
        fifth_b.append(send(g_ref.at[1, x, y], g_ref.at[1, x, y], peer(d, 0, 0)[0]))
        dst_b.append(g_ref.at[1, peer(-d, 0, 0)[1], y])
    land(fifth_a, dst_a)
    sixth_a, sixth_b, end_a, end_b = [], [], [], []
    for d in range(1, nx):
        sixth_a.append(send(g_ref.at[0, x], g_ref.at[0, x], peer(d, 0, 0)[0]))
        end_a.append(g_ref.at[0, peer(-d, 0, 0)[1]])
    land(fifth_b, dst_b)
    for d in range(1, ny):
        sixth_b.append(send(g_ref.at[1, :, y], g_ref.at[1, :, y], peer(0, d, 0)[0]))
        end_b.append(g_ref.at[1, :, peer(0, -d, 0)[2]])
    land(sixth_a, end_a)
    land(sixth_b, end_b)


def reduce_cycle(z, zb, o, n, scale):
    _, _, nx, ny, nz = geometry()
    rows_own = o.shape[0]
    long = nz * rows_own
    copies = 3 * (nx - 1) + 3 * (ny - 1) + 2 * (nz - 1) + (nx - 1) + (ny - 1)
    return pl.pallas_call(
        functools.partial(reduce_kernel, scale),
        out_shape=[jax.ShapeDtypeStruct(o.shape, f32), jax.ShapeDtypeStruct(zb.shape, bf16)],
        in_specs=[VM] * 4,
        out_specs=[VM] * 2,
        scratch_shapes=[
            pltpu.VMEM((ny, long, SG), f32),
            pltpu.VMEM((nx, long, SG), f32),
            pltpu.VMEM((ny, long, SG), bf16),
            pltpu.VMEM((nx, long, SG), bf16),
            pltpu.VMEM((nx - 1, ny, long, SG), bf16),
            pltpu.VMEM((ny - 1, nx, long, SG), bf16),
            pltpu.VMEM((ny - 1, long, SG), bf16),
            pltpu.VMEM((nx - 1, long, SG), bf16),
            pltpu.VMEM((nz, rows_own, 2 * SG), f32),
            pltpu.VMEM((nz, rows_own, 2 * SG), bf16),
            pltpu.VMEM((nz - 1, rows_own, 2 * SG), bf16),
            pltpu.VMEM((nz, rows_own, 2 * SG), bf16),
            pltpu.SemaphoreType.DMA((copies,)),
            pltpu.SemaphoreType.DMA((copies,)),
        ],
        compiler_params=pltpu.CompilerParams(
            collective_id=1, has_side_effects=True, vmem_limit_bytes=LIMIT
        ),
        name="cycle",
    )(z, zb, o, n)


def backward_kernel(scale, g_ref, ar_ref, ai_ref, bt_ref, own_ref, other_ref):
    x, h, y, z = position()
    fs = own_ref.shape[0]
    gr = g_ref[0]
    gi = g_ref[1]
    g = jnp.concatenate([gr, gi], 1)

    def rows(k):
        cut = pl.ds(pl.multiple_of(k * fs, fs), fs)
        first = (((0,), (0,)), ((), ()))
        one = lax.dot_general(ar_ref[:, cut], g, first, preferred_element_type=f32)
        two = lax.dot_general(ai_ref[:, cut], g, first, preferred_element_type=f32)
        u = jnp.concatenate([one[:, :SG] + two[:, SG:], one[:, SG:] - two[:, :SG]], 1).astype(bf16)
        return jnp.dot(u, bt_ref[...], preferred_element_type=f32) * scale

    other_ref[...] = rows(1 - h).astype(bf16)
    own_ref[...] = rows(h)


def backward(g, ar, ai, bt, scale):
    fs = bt.shape[1]
    return pl.pallas_call(
        functools.partial(backward_kernel, scale),
        out_shape=[jax.ShapeDtypeStruct((fs, fs), f32), jax.ShapeDtypeStruct((fs, fs), bf16)],
        in_specs=[VM] * 4,
        out_specs=[VM] * 2,
        compiler_params=pltpu.CompilerParams(vmem_limit_bytes=LIMIT),
        name="backward",
    )(g, ar, ai, bt)


def last_kernel(other_ref, vals_ref, got_ref, sums_ref, slots, lsem, ssem, rsem, vs, vr):
    rows, cols, _, _, _ = geometry()
    frow = lax.axis_index("frow")
    fcol = lax.axis_index("fcol")
    h = frow % 2
    n = rows * cols
    me = frow * cols + fcol
    greet_all(n, cols, me)
    sib = frow + 1 - 2 * h
    big = pltpu.make_async_remote_copy(
        other_ref, got_ref, ssem, rsem, device_id=(sib, fcol), device_id_type=MESH
    )
    big.start()

    def link(d, to, slot):
        return pltpu.make_async_remote_copy(
            vals_ref.at[to], slots.at[slot], vs.at[d], vr.at[d],
            device_id=(to // cols, to % cols), device_id_type=MESH,
        )

    everyone(n, cols, me, lambda d, to, frm: link(d, to, me).start())
    mine = pltpu.make_async_copy(vals_ref.at[me], slots.at[me], lsem)
    mine.start()
    mine.wait()
    everyone(n, cols, me, lambda d, to, frm: link(d, to, me).wait_send())
    everyone(n, cols, me, lambda d, to, frm: link(d, to, frm).wait_recv())
    sums_ref[...] = lax.fori_loop(1, n, lambda k, t: t + slots[k], slots[0])
    big.wait()


def last(other, vals):
    rows, cols, _, _, _ = geometry()
    n = rows * cols
    return pl.pallas_call(
        last_kernel,
        out_shape=[
            jax.ShapeDtypeStruct(other.shape, bf16),
            jax.ShapeDtypeStruct(vals.shape[1:], f32),
        ],
        in_specs=[VM, VM],
        out_specs=[VM, VM],
        scratch_shapes=[
            pltpu.VMEM(vals.shape, f32),
            pltpu.SemaphoreType.DMA,
            pltpu.SemaphoreType.DMA,
            pltpu.SemaphoreType.DMA,
            pltpu.SemaphoreType.DMA((n,)),
            pltpu.SemaphoreType.DMA((n,)),
        ],
        compiler_params=pltpu.CompilerParams(
            collective_id=2, has_side_effects=True, vmem_limit_bytes=LIMIT
        ),
        name="last",
    )(other, vals)


def shards(facet_image, row_offsets, col_offsets, vis_subgrid, vis_u, vis_v, observed):
    rows, cols, nx, ny, nz = geometry()
    fs = facet_image.shape[0]
    rows_own = NR * SG // (nx * ny * nz)
    scale_in = 1.0 / (fs * math.sqrt(rows * cols))
    scale_out = 1.0 / (SG * math.sqrt(NR * NC))
    cell = ((vis_subgrid * SG + vis_u) * SG + vis_v).astype(f32)
    vis = jnp.concatenate([cell[None], observed, jnp.zeros_like(cell)[None]], 0)
    pair, vis_all = swap(facet_image, vis)
    ar, ai, bt = tables(fs, row_offsets, col_offsets)
    z, zb = forward(pair, ar, ai, bt)
    o, n = gridding(vis_all, rows_own)
    m, g = reduce_cycle(z, zb, o, n, scale_in / SG)
    vals = degrid(m, vis_all)
    own, other = backward(g.reshape(2, NR * SG, SG), ar, ai, bt, scale_out / SG)
    got, sums = last(other, vals)
    return (own + got.astype(f32), observed - sums)


def solution(mesh):
    in_specs = (
        P("frow", "fcol"),
        P(),
        P(),
        P(("frow", "fcol")),
        P(("frow", "fcol")),
        P(("frow", "fcol")),
        P(None, ("frow", "fcol")),
    )
    out_specs = (P("frow", "fcol"), P(None, ("frow", "fcol")))
    return jax.shard_map(shards, mesh=mesh, in_specs=in_specs, out_specs=out_specs, check_vma=False)
```

time: 195 us -> 98.2 us (0.50)
  blocking collectives: 127 us -> 0 us
  Pallas kernels: 0 us -> 92.3 us
  other arithmetic: 28.6 us -> 3.44 us
  matrix products: 20.3 us -> 0 us
  local copies, waits for them, and re-layouts: 17.1 us -> 1.39 us
    psum x2 -> x0, blocking collectives: 127 us -> none  [the longest x1 64.4 us: shards(): summed = lax.psum(stacked, ('frow', 'fcol'))]
    pallas_call x0 -> x8, Pallas kernels: none -> 92.3 us  [the longest x1 30.2 us: reduce_cycle(): pl.pallas_call(functools.partial(reduce_kernel, scale), out_shape=[jax.Sh...]
    dot_general x16 -> x0, matrix products: 20.3 us -> none  [the longest x2 6.29 us: shards(): jnp.dot(u_both.astype(bf16), jnp.concatenate([col_cos, -col_sin], 0), pre...]
    convert_element_type x4 -> x1, other arithmetic: 10.8 us -> 0.01 us  [shards(): cell = ((vis_subgrid * SG + vis_u) * SG + vis_v).astype(f32)]
    gather x2 -> x0, local copies, waits for them, and re-layouts: 7.41 us -> none  [the longest x1 4.27 us: shards(): jnp.take(hat_imag.reshape(-1), cell_ids)]
    scatter-add x2 -> x0, other arithmetic: 7.18 us -> none  [the longest x1 3.66 us: shards(): jax.ops.segment_sum(residual[1], cell_ids, num_segments=cells_all)]
    neg x3 -> x0, other arithmetic: 5.39 us -> none  [the longest x1 4.36 us: shards(): -col_sin]
    select_n x8 -> x0, other arithmetic: 3.25 us -> none  [the longest x4 2.63 us: wrapped(): low_part = frequency % 256]
where the time goes in v1:
time: 98.2 us; the launch traced here: 97.8 us
  Pallas kernels  92.3 us (94%)
  other arithmetic  3.44 us (4%)
  local copies, waits for them, and re-layouts  1.39 us (1%)
    pallas_call x1, Pallas kernels, reduce_cycle(): pl.pallas_call(functools.partial(reduce_kernel, scale), out_shape=[jax.Sh...  30.2 us
    pallas_call x1, Pallas kernels, swap(): pl.pallas_call(swap_kernel, out_shape=[jax.ShapeDtypeStruct((2,) + facet....  16.6 us
    pallas_call x1, Pallas kernels, last(): pl.pallas_call(last_kernel, out_shape=[jax.ShapeDtypeStruct(other.shape,...  10.7 us
    pallas_call x1, Pallas kernels, degrid(): pl.pallas_call(functools.partial(degrid_kernel, m.shape[0]), out_shape=ja...  10.1 us
    pallas_call x1, Pallas kernels, gridding(): pl.pallas_call(functools.partial(grid_kernel, rows_own), out_shape=[shape...  9.7 us
    pallas_call x1, Pallas kernels, backward(): pl.pallas_call(functools.partial(backward_kernel, scale), out_shape=[jax....  5.23 us
    pallas_call x1, Pallas kernels, forward(): pl.pallas_call(functools.partial(forward_kernel, nx, ny), out_shape=[jax....  5.02 us
    pallas_call x1, Pallas kernels, tables(): pl.pallas_call(functools.partial(tables_kernel, fs), out_shape=[jax.Shape...  4.87 us

profile of v1, /device:TPU:0, one launch (start us, length us, event | category | flops | bytes accessed | tf_op | source)
XLA Modules:
  0.0 97.8 jit_solution(12419601512952349047)
XLA Ops:
  0.6 0.0 copy-start.5
  0.6 4.9 %tables.1 = (bf16[512,1024]{1,0:T(8,128)(2,1)}, bf16[512,1024]{1,0:T(8,128)(2,1)}, bf16[512,512]{1,0:T(8,128)(2,1)}) custom-call(s32[2]{0:T(128)} %ro_ref.1, s32[2]{0:T(128)} %co_ref.1), custom_call_target="tpu_custom_call" | custom-call | tf_op jit(solution)/shard_map/tables/pallas_call | solution.py:92
  5.5 0.0 copy-start.4
  5.5 0.0 copy-start.3
  5.5 0.0 copy-done.5
  5.5 0.7 copy-done.4
  6.2 0.0 copy-done.3
  6.2 0.0 copy-start.1
  6.2 0.1 pad.2.clone
  6.3 0.6 copy-done.1
  6.9 0.7 maximum_maximum_fusion.vis_ref
  7.6 16.6 %swap.1 = (bf16[2,512,512]{2,1,0:T(8,128)(2,1)}, f32[32,4,512]{2,1,0:T(4,128)}) custom-call(bf16[512,512]{1,0:T(8,128)(2,1)} %facet_ref.1, f32[4,512]{1,0:T(4,128)} %maximum_maximum_fusion.vis_ref), custom_call_target="tpu_custom_call" | custom-call | tf_op jit(solution)/shard_map/swap/pallas_call | solution.py:170
  24.1 5.0 %forward.1 = (f32[2,2,2,128,256]{4,3,2,1,0:T(8,128)}, bf16[2,2,2,128,256]{4,3,2,1,0:T(8,128)(2,1)}) custom-call(bf16[2,512,512]{2,1,0:T(8,128)(2,1)} %get-tuple-element.17.pair_ref, bf16[512,1024]{1,0:T(8,128)(2,1)} %get-tuple-element.18.ar_ref, bf16[512,1024]{1,0:T(8,128)(2,1)} %get-tuple-element.19.ai_ref, bf16[512,512]{1,0:T(8,128)(2,1)} %get-tuple-element.20.bt_ref), custom_call_target="tpu_custom_call" | custom-call | tf_op jit(solution)/shard_map/forward/pallas_call | solution.py:213
  29.2 9.7 %gridding.1 = (f32[32,512]{1,0:T(8,128)}, f32[32,512]{1,0:T(8,128)}) custom-call(f32[32,4,512]{2,1,0:T(4,128)} %get-tuple-element.23.all_ref), custom_call_target="tpu_custom_call" | custom-call | tf_op jit(solution)/shard_map/gridding/pallas_call | solution.py:264
  38.9 30.2 %cycle.1 = (f32[32,512]{1,0:T(8,128)}, bf16[2,2,2,128,256]{4,3,2,1,0:T(8,128)(2,1)}) custom-call(f32[2,2,2,128,256]{4,3,2,1,0:T(8,128)} %get-tuple-element.21.z_ref, bf16[2,2,2,128,256]{4,3,2,1,0:T(8,128)(2,1)} %get-tuple-element.22.zb_ref, f32[32,512]{1,0:T(8,128)} %get-tuple-element.24.o_ref, f32[32,512]{1,0:T(8,128)} %get-tuple-element.25.n_ref), custom_call_target="tpu_custom_call" | custom-call | tf_op jit(solution)/shard_map/cycle/pallas_call | solution.py:434
  69.1 5.2 %backward.1 = (f32[512,512]{1,0:T(8,128)}, bf16[512,512]{1,0:T(8,128)(2,1)}) custom-call(bf16[2,512,256]{2,1,0:T(8,128)(2,1)} %bitcast.3, bf16[512,1024]{1,0:T(8,128)(2,1)} %get-tuple-element.18.ar_ref, bf16[512,1024]{1,0:T(8,128)(2,1)} %get-tuple-element.19.ai_ref, bf16[512,512]{1,0:T(8,128)(2,1)} %get-tuple-element.20.bt_ref), custom_call_target="tpu_custom_call" | custom-call | tf_op jit(solution)/shard_map/backward/pallas_call | solution.py:483
  74.3 0.0 copy-start
  74.3 10.1 %degrid.1.vals_ref = f32[32,2,512]{2,1,0:T(2,128)} custom-call(f32[32,512]{1,0:T(8,128)} %get-tuple-element.29.m_ref, f32[32,4,512]{2,1,0:T(4,128)} %get-tuple-element.23.all_ref), custom_call_target="tpu_custom_call" | custom-call | tf_op jit(solution)/shard_map/degrid/pallas_call | solution.py:295
  84.4 10.7 %last.1 = (bf16[512,512]{1,0:T(8,128)(2,1)}, f32[2,512]{1,0:T(2,128)}) custom-call(bf16[512,512]{1,0:T(8,128)(2,1)} %get-tuple-element.28.other_ref, f32[32,2,512]{2,1,0:T(2,128)} %degrid.1.vals_ref), custom_call_target="tpu_custom_call" | custom-call | tf_op jit(solution)/shard_map/last/pallas_call | solution.py:526
  95.1 0.0 copy-done
  95.1 0.0 copy-start.2
  95.1 2.2 %convert_add_fusion = f32[512,512]{1,0:T(8,128)} fusion(f32[512,512]{1,0:T(8,128)S(1)} %copy-done, bf16[512,512]{1,0:T(8,128)(2,1)} %get-tuple-element.30), kind=kLoop, calls=%fused_computation | loop fusion | flops 524288 | bytes 2621440 | tf_op jit(solution)/shard_map/add | solution.py:565
  97.2 0.0 copy-done.2
  97.3 0.6 sub.3
  (1 shorter events, 0.0 us)
Async XLA Ops:
  0.6 4.9 %copy-start.5 = (s32[512]{0:T(512)S(1)}, s32[512]{0:T(512)}, u32[]{:S(2)}) copy-start(s32[512]{0:T(512)} %param.10) | copy-start | bytes 6148
  5.5 0.7 copy-start.4
  5.5 0.7 copy-start.3
  6.2 0.7 copy-start.1
  74.3 20.8 %copy-start = (f32[512,512]{1,0:T(8,128)S(1)}, f32[512,512]{1,0:T(8,128)}, u32[]{:S(2)}) copy-start(f32[512,512]{1,0:T(8,128)} %get-tuple-element.27) | copy-start | bytes 3145732
  95.1 2.2 %copy-start.2 = (f32[2,512]{1,0:T(2,128)S(1)}, f32[2,512]{1,0:T(2,128)}, u32[]{:S(2)}) copy-start(f32[2,512]{1,0:T(2,128)} %get-tuple-element.31) | copy-start | bytes 12292

commit v2 on v0

v2 whole, which is shorter than its diff:
```python
import functools
import math

import jax
import jax.numpy as jnp
from jax import lax
from jax.experimental import pallas as pl
from jax.experimental.pallas import tpu as pltpu
from jax.sharding import PartitionSpec as P

SKY = 65536
SG = 256
NR = 2
NC = 2
f32 = jnp.float32
bf16 = jnp.bfloat16
i32 = jnp.int32
MESH = pl.DeviceIdType.MESH
VM = pl.BlockSpec(memory_space=pltpu.VMEM)
SM = pl.BlockSpec(memory_space=pltpu.SMEM)
LIMIT = 60 << 20


def geometry():
    rows = lax.axis_size("frow")
    cols = lax.axis_size("fcol")
    nx = rows // 2
    ny = 1 << ((cols.bit_length() - 1) // 2)
    nz = cols // ny
    return rows, cols, nx, ny, nz


def position():
    _, _, _, ny, _ = geometry()
    frow = lax.axis_index("frow")
    fcol = lax.axis_index("fcol")
    return frow // 2, frow % 2, fcol % ny, fcol // ny


def dims(contract):
    return ((contract, contract), ((), ()))


def phase(product):
    angle = (product & (SKY - 1)).astype(f32) * (2.0 * math.pi / SKY)
    return jnp.cos(angle), jnp.sin(angle)


def expand(first, places, c_ref, s_ref):
    n = places.shape[1]
    steps = lax.broadcasted_iota(i32, (16, n), 0)
    c0, s0 = phase(steps * places)
    c1, s1 = phase((first + 16 * steps) * places)
    for k in range(SG // 16):
        ck = c1[k : k + 1]
        sk = s1[k : k + 1]
        c_ref[k * 16 : k * 16 + 16, :] = (ck * c0 - sk * s0).astype(bf16)
        s_ref[k * 16 : k * 16 + 16, :] = (sk * c0 + ck * s0).astype(bf16)


def place(q):
    _, _, _, ny, nz = geometry()
    return q // (ny * nz), (q // nz) % ny, q % nz


def device(q, h):
    _, _, _, ny, _ = geometry()
    x, y, z = place(q)
    return (2 * x + h, z * ny + y)


def hots(vis, h, base, rows_own):
    n = vis.shape[1]
    cell = vis[0:1].astype(i32)
    sub = cell // (SG * SG)
    row = (sub // NC) * SG + (cell // SG) % SG - base
    row = jnp.where(sub % NC == h, row, -1)
    hot_row = lax.broadcasted_iota(i32, (rows_own, n), 0) == row
    hot_col = lax.broadcasted_iota(i32, (SG, n), 0) == cell % SG
    return hot_row, jnp.where(hot_col, 1.0, 0.0).astype(bf16)


def main_kernel(
    scale, ro_ref, co_ref, sub_ref, u_ref, v_ref, obs_ref, facet_ref,
    g_ref, ar_ref, ai_ref, bt_ref, res_ref,
    kk, ks, rc, rs, vis_ref, vis_all, other, z_ref, zb_ref, grid_acc,
    acc_a, acc_b, send_a, send_b, got_a1, got_b1, got_a2, got_b2,
    own_z, send_z, got_z, gz, model, vals, pair_vals, slots,
    ssem, rsem, vs, vr, ws, wr, lsem,
):
    rows, cols, nx, ny, nz = geometry()
    x, h, y, z = position()
    chips = nx * ny * nz
    me = (x * ny + y) * nz + z
    fs = facet_ref.shape[0]
    nv = vis_ref.shape[1]
    rows_own = NR * SG // chips
    sib = (2 * x + 1 - h, lax.axis_index("fcol"))
    barrier = pltpu.get_barrier_semaphore()

    def peers(act):
        def step(d, carry):
            act(d, lax.rem(me + d, chips), lax.rem(me - d + chips, chips))
            return carry

        lax.fori_loop(1, chips, step, 0)

    peers(lambda d, to, frm: pl.semaphore_signal(barrier, inc=1, device_id=device(to, h), device_id_type=MESH))
    pl.semaphore_signal(barrier, inc=1, device_id=sib, device_id_type=MESH)
    cell = (sub_ref[...] * SG + u_ref[...]) * SG + v_ref[...]
    vis_ref[0:1] = cell.astype(f32)
    vis_ref[1:3] = obs_ref[...]
    vis_ref[3:4] = jnp.zeros((1, nv), f32)
    mine = pltpu.make_async_copy(vis_ref, vis_all.at[h, me], lsem)
    mine.start()
    expand(0, lax.broadcasted_iota(i32, (1, SG), 1) * (SKY // SG), kk, ks)
    pl.semaphore_wait(barrier, chips)
    used = [0]
    sent = []

    def send(src, dst, to):
        k = used[0]
        used[0] += 1
        copy = pltpu.make_async_remote_copy(
            src, dst, ssem.at[k], rsem.at[k], device_id=to, device_id_type=MESH
        )
        copy.start()
        sent.append(copy)
        return k

    def land(k, dst):
        pltpu.make_async_remote_copy(
            dst, dst, ssem.at[k], rsem.at[k], device_id=sib, device_id_type=MESH
        ).wait_recv()

    def link(d, to, slot):
        return pltpu.make_async_remote_copy(
            vis_ref, vis_all.at[h, slot], vs.at[d], vr.at[d],
            device_id=device(to, h), device_id_type=MESH,
        )

    k_facet = send(facet_ref, other, sib)
    peers(lambda d, to, frm: link(d, to, me).start())

    kcos = kk[...]
    ksin = ks[...]

    def compose(n):
        c = rc[:, :n]
        s = rs[:, :n]
        re = jnp.dot(kcos, c, preferred_element_type=f32) + jnp.dot(ksin, s, preferred_element_type=f32)
        im = jnp.dot(ksin, c, preferred_element_type=f32) - jnp.dot(kcos, s, preferred_element_type=f32)
        return re.astype(bf16), im.astype(bf16)

    step = SKY // (cols * fs)
    places = (lax.axis_index("fcol") * fs + lax.broadcasted_iota(i32, (1, fs), 1)) * step
    for c in range(NC):
        expand(co_ref[c], places, rc.at[:, :fs], rs.at[:, :fs])
        re, im = compose(fs)
        bt_ref[c, :SG] = re
        bt_ref[c, SG:] = im
    step = SKY // (rows * fs)
    places = (x * (2 * fs) + lax.broadcasted_iota(i32, (1, 2 * fs), 1)) * step
    for r in range(NR):
        expand(ro_ref[r], places, rc, rs)
        re, im = compose(2 * fs)
        ar_ref[r * SG : r * SG + SG] = re
        ai_ref[r * SG : r * SG + SG] = im

    mine.wait()
    bt = bt_ref[h]

    def project(ref):
        return lax.dot_general(ref[...], bt, (((1,), (1,)), ((), ())), preferred_element_type=f32).astype(bf16)

    own_p = project(facet_ref)
    peers(lambda d, to, frm: link(d, to, frm).wait_recv())
    k_vis = send(vis_all.at[h], vis_all.at[h], sib)
    land(k_facet, other)
    other_p = project(other)
    part = NR * SG // (nx * ny)
    own_cut = pl.ds(pl.multiple_of(h * fs, fs), fs)
    other_cut = pl.ds(pl.multiple_of((1 - h) * fs, fs), fs)
    first_a, first_b = [], []
    for dx in list(range(1, nx)) + [0]:
        px = lax.rem(x + dx, nx)
        for dy in list(range(1, ny)) + [0]:
            py = lax.rem(y + dy, ny)
            cut = pl.ds(pl.multiple_of((px * ny + py) * part, part), part)
            one = jnp.dot(ar_ref[cut, own_cut], own_p, preferred_element_type=f32)
            one += jnp.dot(ar_ref[cut, other_cut], other_p, preferred_element_type=f32)
            two = jnp.dot(ai_ref[cut, own_cut], own_p, preferred_element_type=f32)
            two += jnp.dot(ai_ref[cut, other_cut], other_p, preferred_element_type=f32)
            zr = one[:, :SG] - two[:, SG:]
            zi = one[:, SG:] + two[:, :SG]
            z_ref[0, px, py] = zr
            z_ref[1, px, py] = zi
            zb_ref[0, px, py] = zr.astype(bf16)
            zb_ref[1, px, py] = zi.astype(bf16)
            if dx == 0 and dy > 0:
                first_b.append(send(zb_ref.at[1, :, py], got_b1.at[dy - 1], device((x * ny + py) * nz + z, h)))
        if dx > 0:
            first_a.append(send(zb_ref.at[0, px], got_a1.at[dx - 1], device((px * ny + y) * nz + z, h)))

    base = me * rows_own
    grid_acc[...] = jnp.zeros_like(grid_acc)

    def gridding(side, lo, hi):
        def one(q):
            vis = vis_all[side, q]
            hot_row, hot_col = hots(vis, h, base, rows_own)
            parts = []
            for p in (1, 2):
                val = vis[p : p + 1]
                high = val.astype(bf16).astype(f32)
                parts += [high, val - high]
            parts.append(jnp.ones_like(vis[0:1]))
            left = jnp.concatenate([jnp.where(hot_row, t, 0.0) for t in parts], 0).astype(bf16)
            return lax.dot_general(left, hot_col, (((1,), (1,)), ((), ())), preferred_element_type=f32)

        def body(t, carry):
            got = one(lo + 2 * t) + one(lo + 2 * t + 1)
            grid_acc[...] += got
            return carry

        lax.fori_loop(0, (hi - lo) // 2, body, 0)

    half = chips // 2
    gridding(h, 0, half + half // 2)
    for k, dst in zip(first_a, range(nx - 1)):
        land(k, got_a1.at[dst])
    total = z_ref[0, x]
    for d in range(nx - 1):
        total = total + got_a1[d].astype(f32)
    acc_a[...] = total
    send_a[...] = total.astype(bf16)
    second_a, second_b = [], []
    for d in range(1, ny):
        py = lax.rem(y + d, ny)
        second_a.append(send(send_a.at[py], got_a2.at[d - 1], device((x * ny + py) * nz + z, h)))
    for k, dst in zip(first_b, range(ny - 1)):
        land(k, got_b1.at[dst])
    total = z_ref[1, :, y]
    for d in range(ny - 1):
        total = total + got_b1[d].astype(f32)
    acc_b[...] = total
    send_b[...] = total.astype(bf16)
    for d in range(1, nx):
        px = lax.rem(x + d, nx)
        second_b.append(send(send_b.at[px], got_b2.at[d - 1], device((px * ny + y) * nz + z, h)))
    gridding(h, half + half // 2, chips)
    land(k_vis, vis_all.at[1 - h])
    gridding(1 - h, 0, half // 2)
    for k, dst in zip(second_a, range(ny - 1)):
        land(k, got_a2.at[dst])
    re = acc_a[y]
    for d in range(ny - 1):
        re = re + got_a2[d].astype(f32)
    for k, dst in zip(second_b, range(nx - 1)):
        land(k, got_b2.at[dst])
    im = acc_b[x]
    for d in range(nx - 1):
        im = im + got_b2[d].astype(f32)
    for k in range(nz):
        cut = slice(k * rows_own, (k + 1) * rows_own)
        own_z[k, :, :SG] = re[cut]
        own_z[k, :, SG:] = im[cut]
        send_z[k, :, :SG] = re[cut].astype(bf16)
        send_z[k, :, SG:] = im[cut].astype(bf16)
    third = []
    for d in range(1, nz):
        pz = lax.rem(z + d, nz)
        third.append(send(send_z.at[pz], got_z.at[d - 1], device((x * ny + y) * nz + pz, h)))
    gridding(1 - h, half // 2, chips)
    for k, dst in zip(third, range(nz - 1)):
        land(k, got_z.at[dst])
    total = own_z[z]
    for d in range(nz - 1):
        total = total + got_z[d].astype(f32)
    m = total * scale
    got = [grid_acc[p * rows_own : (p + 1) * rows_own] for p in range(5)]
    hat_re = got[0] + got[1] - got[4] * m[:, :SG]
    hat_im = got[2] + got[3] - got[4] * m[:, SG:]
    gz[z, :, :SG] = hat_re.astype(bf16)
    gz[z, :, SG:] = hat_im.astype(bf16)
    fourth = []
    for d in range(1, nz):
        pz = lax.rem(z + d, nz)
        fourth.append(send(gz.at[z], gz.at[z], device((x * ny + y) * nz + pz, h)))
    both = jnp.concatenate([m[:, :SG], m[:, SG:]], 0)
    high = both.astype(bf16)
    model[: 2 * rows_own] = high
    model[2 * rows_own :] = (both - high.astype(f32)).astype(bf16)

    def degrid(side, lo, hi):
        def one(q):
            hot_row, hot_col = hots(vis_all[side, q], h, base, rows_own)
            val = jnp.dot(model[...], hot_col, preferred_element_type=f32)
            val = val[: 2 * rows_own] + val[2 * rows_own :]
            vr_ = jnp.sum(jnp.where(hot_row, val[:rows_own], 0.0), 0, keepdims=True)
            vi_ = jnp.sum(jnp.where(hot_row, val[rows_own:], 0.0), 0, keepdims=True)
            return jnp.concatenate([vr_, vi_], 0)

        def body(t, carry):
            a = one(lo + 2 * t)
            b = one(lo + 2 * t + 1)
            vals[side, lo + 2 * t] = a
            vals[side, lo + 2 * t + 1] = b
            return carry

        lax.fori_loop(0, (hi - lo) // 2, body, 0)

    degrid(1 - h, 0, chips)
    k_vals = send(vals.at[1 - h], pair_vals, sib)
    for k, d in zip(fourth, range(1, nz)):
        land(k, gz.at[lax.rem(z - d + nz, nz)])
    for k in range(nz):
        cut = slice(k * rows_own, (k + 1) * rows_own)
        g_ref[h, 0, x, y, cut, :] = gz[k, :, :SG]
        g_ref[h, 1, x, y, cut, :] = gz[k, :, SG:]
    fifth_a, fifth_b, cross = [], [], []

    def over(index):
        src = g_ref.at[(h,) + index]
        cross.append((send(src, src, sib), index))

    for d in range(1, ny):
        blk = g_ref.at[h, 0, x, y]
        fifth_a.append(send(blk, blk, device((x * ny + lax.rem(y + d, ny)) * nz + z, h)))
    for d in range(1, nx):
        blk = g_ref.at[h, 1, x, y]
        fifth_b.append(send(blk, blk, device((lax.rem(x + d, nx) * ny + y) * nz + z, h)))
    over((0, x, y))
    over((1, x, y))
    degrid(h, 0, half)
    for k, d in zip(fifth_a, range(1, ny)):
        land(k, g_ref.at[h, 0, x, lax.rem(y - d + ny, ny)])
    sixth_a, sixth_b = [], []
    for d in range(1, nx):
        blk = g_ref.at[h, 0, x]
        sixth_a.append(send(blk, blk, device((lax.rem(x + d, nx) * ny + y) * nz + z, h)))
    for k, d in zip(fifth_b, range(1, nx)):
        land(k, g_ref.at[h, 1, lax.rem(x - d + nx, nx), y])
    for d in range(1, ny):
        blk = g_ref.at[h, 1, :, y]
        sixth_b.append(send(blk, blk, device((x * ny + lax.rem(y + d, ny)) * nz + z, h)))
    for d in range(1, ny):
        over((0, x, lax.rem(y - d + ny, ny)))
    for d in range(1, nx):
        over((1, lax.rem(x - d + nx, nx), y))
    degrid(h, half, chips)
    land(k_vals, pair_vals)
    vals[h] = vals[h] + pair_vals[...]

    def back(d, to, slot):
        return pltpu.make_async_remote_copy(
            vals.at[h, to], slots.at[slot], ws.at[d], wr.at[d],
            device_id=device(to, h), device_id_type=MESH,
        )

    peers(lambda d, to, frm: back(d, to, me).start())
    for k, d in zip(sixth_a, range(1, nx)):
        px = lax.rem(x - d + nx, nx)
        land(k, g_ref.at[h, 0, px])
        over((0, px))
    for k, d in zip(sixth_b, range(1, ny)):
        py = lax.rem(y - d + ny, ny)
        land(k, g_ref.at[h, 1, :, py])
        over((1, slice(None), py))
    peers(lambda d, to, frm: back(d, to, frm).wait_recv())
    start = vals[h, me]
    res_ref[...] = obs_ref[...] - lax.fori_loop(
        1, chips, lambda d, t: t + slots[lax.rem(me + d, chips)], start
    )
    for k, index in cross:
        land(k, g_ref.at[(1 - h,) + index])
    for copy in sent:
        copy.wait_send()
    peers(lambda d, to, frm: link(d, to, me).wait_send())
    peers(lambda d, to, frm: back(d, to, me).wait_send())


def main(ro, co, sub, u, v, obs, facet, scale):
    _, _, nx, ny, nz = geometry()
    chips = nx * ny * nz
    fs = facet.shape[0]
    nv = obs.shape[1]
    rows_own = NR * SG // chips
    long = nz * rows_own
    copies = 64
    dma = pltpu.SemaphoreType.DMA
    return pl.pallas_call(
        functools.partial(main_kernel, scale),
        out_shape=[
            jax.ShapeDtypeStruct((2, 2, nx, ny, long, SG), bf16),
            jax.ShapeDtypeStruct((NR * SG, 2 * fs), bf16),
            jax.ShapeDtypeStruct((NR * SG, 2 * fs), bf16),
            jax.ShapeDtypeStruct((NC, 2 * SG, fs), bf16),
            jax.ShapeDtypeStruct((2, nv), f32),
        ],
        in_specs=[SM, SM] + [VM] * 5,
        out_specs=[VM] * 5,
        scratch_shapes=[
            pltpu.VMEM((SG, SG), bf16),
            pltpu.VMEM((SG, SG), bf16),
            pltpu.VMEM((SG, 2 * fs), bf16),
            pltpu.VMEM((SG, 2 * fs), bf16),
            pltpu.VMEM((4, nv), f32),
            pltpu.VMEM((2, chips, 4, nv), f32),
            pltpu.VMEM((fs, fs), bf16),
            pltpu.VMEM((2, nx, ny, long, SG), f32),
            pltpu.VMEM((2, nx, ny, long, SG), bf16),
            pltpu.VMEM((5 * rows_own, SG), f32),
            pltpu.VMEM((ny, long, SG), f32),
            pltpu.VMEM((nx, long, SG), f32),
            pltpu.VMEM((ny, long, SG), bf16),
            pltpu.VMEM((nx, long, SG), bf16),
            pltpu.VMEM((nx - 1, ny, long, SG), bf16),
            pltpu.VMEM((ny - 1, nx, long, SG), bf16),
            pltpu.VMEM((ny - 1, long, SG), bf16),
            pltpu.VMEM((nx - 1, long, SG), bf16),
            pltpu.VMEM((nz, rows_own, 2 * SG), f32),
            pltpu.VMEM((nz, rows_own, 2 * SG), bf16),
            pltpu.VMEM((nz - 1, rows_own, 2 * SG), bf16),
            pltpu.VMEM((nz, rows_own, 2 * SG), bf16),
            pltpu.VMEM((4 * rows_own, SG), bf16),
            pltpu.VMEM((2, chips, 2, nv), f32),
            pltpu.VMEM((chips, 2, nv), f32),
            pltpu.VMEM((chips, 2, nv), f32),
            dma((copies,)),
            dma((copies,)),
            dma((chips,)),
            dma((chips,)),
            dma((chips,)),
            dma((chips,)),
            dma,
        ],
        compiler_params=pltpu.CompilerParams(
            collective_id=0, has_side_effects=True, vmem_limit_bytes=LIMIT
        ),
        name="cycle",
    )(ro, co, sub, u, v, obs, facet)


def backward_kernel(scale, g_ref, ar_ref, ai_ref, bt_ref, image_ref):
    _, h, _, _ = position()
    fs = image_ref.shape[0]
    cut = pl.ds(pl.multiple_of(h * fs, fs), fs)
    first = (((0,), (0,)), ((), ()))
    g = jnp.concatenate([g_ref[c, p] for c in range(NC) for p in range(2)], 1)
    one = lax.dot_general(ar_ref[:, cut], g, first, preferred_element_type=f32)
    two = lax.dot_general(ai_ref[:, cut], g, first, preferred_element_type=f32)
    parts = []
    for c in range(NC):
        re = slice(2 * c * SG, (2 * c + 1) * SG)
        im = slice((2 * c + 1) * SG, (2 * c + 2) * SG)
        parts += [one[:, re] + two[:, im], one[:, im] - two[:, re]]
    u = jnp.concatenate(parts, 1).astype(bf16)
    b = bt_ref[...].reshape(2 * NC * SG, fs)
    image_ref[...] = jnp.dot(u, b, preferred_element_type=f32) * scale


def backward(g, ar, ai, bt, scale):
    fs = bt.shape[2]
    return pl.pallas_call(
        functools.partial(backward_kernel, scale),
        out_shape=jax.ShapeDtypeStruct((fs, fs), f32),
        in_specs=[VM] * 4,
        out_specs=VM,
        compiler_params=pltpu.CompilerParams(vmem_limit_bytes=LIMIT),
        name="backward",
    )(g, ar, ai, bt)


def shards(facet_image, row_offsets, col_offsets, vis_subgrid, vis_u, vis_v, observed):
    rows, cols, _, _, _ = geometry()
    fs = facet_image.shape[0]
    scale_in = 1.0 / (fs * math.sqrt(rows * cols))
    scale_out = 1.0 / (SG * math.sqrt(NR * NC))
    g, ar, ai, bt, residual = main(
        row_offsets, col_offsets, vis_subgrid[None], vis_u[None], vis_v[None],
        observed, facet_image, scale_in / SG,
    )
    image = backward(g.reshape(NC, 2, NR * SG, SG), ar, ai, bt, scale_out / SG)
    return (image, residual)


def solution(mesh):
    in_specs = (
        P("frow", "fcol"),
        P(),
        P(),
        P(("frow", "fcol")),
        P(("frow", "fcol")),
        P(("frow", "fcol")),
        P(None, ("frow", "fcol")),
    )
    out_specs = (P("frow", "fcol"), P(None, ("frow", "fcol")))
    return jax.shard_map(shards, mesh=mesh, in_specs=in_specs, out_specs=out_specs, check_vma=False)
```

time: 195 us -> 51.1 us (0.26)
  blocking collectives: 127 us -> 0 us
  Pallas kernels: 0 us -> 49.7 us
  other arithmetic: 28.6 us -> 0 us
  matrix products: 20.3 us -> 0 us
  local copies, waits for them, and re-layouts: 17.1 us -> 0.6 us
    psum x2 -> x0, blocking collectives: 127 us -> none  [the longest x1 64.4 us: shards(): summed = lax.psum(stacked, ('frow', 'fcol'))]
    pallas_call x0 -> x2, Pallas kernels: none -> 49.7 us  [the longest x1 44.7 us: main(): pl.pallas_call(functools.partial(main_kernel, scale), out_shape=[jax.Shap...]
    dot_general x16 -> x0, matrix products: 20.3 us -> none  [the longest x2 6.29 us: shards(): jnp.dot(u_both.astype(bf16), jnp.concatenate([col_cos, -col_sin], 0), pre...]
    convert_element_type x4 -> x0, other arithmetic: 10.8 us -> none  [the longest x1 4.64 us: sky_tables(): jnp.sin(angles).astype(jnp.bfloat16)]
    gather x2 -> x0, local copies, waits for them, and re-layouts: 7.41 us -> none  [the longest x1 4.27 us: shards(): jnp.take(hat_imag.reshape(-1), cell_ids)]
    scatter-add x2 -> x0, other arithmetic: 7.18 us -> none  [the longest x1 3.66 us: shards(): jax.ops.segment_sum(residual[1], cell_ids, num_segments=cells_all)]
    neg x3 -> x0, other arithmetic: 5.39 us -> none  [the longest x1 4.36 us: shards(): -col_sin]
    select_n x8 -> x0, other arithmetic: 3.25 us -> none  [the longest x4 2.63 us: wrapped(): low_part = frequency % 256]
where the time goes in v2:
time: 51.1 us; the launch traced here: 50.9 us
  Pallas kernels  49.7 us (97%)
  between operations  0.65 us (1%)
  local copies, waits for them, and re-layouts  0.6 us (1%)
    pallas_call x1, Pallas kernels, main(): pl.pallas_call(functools.partial(main_kernel, scale), out_shape=[jax.Shap...  44.7 us
    pallas_call x1, Pallas kernels, backward(): pl.pallas_call(functools.partial(backward_kernel, scale), out_shape=jax.S...  4.99 us

profile of v2, /device:TPU:0, one launch (start us, length us, event | category | flops | bytes accessed | tf_op | source)
XLA Modules:
  0.0 50.9 jit_solution(7602259215987153159)
XLA Ops:
  0.6 44.7 %cycle.1 = (bf16[2,2,2,2,128,256]{5,4,3,2,1,0:T(8,128)(2,1)}, bf16[512,1024]{1,0:T(8,128)(2,1)}, bf16[512,1024]{1,0:T(8,128)(2,1)}, bf16[2,512,512]{2,1,0:T(8,128)(2,1)}, f32[2,512]{1,0:T(2,128)}) custom-call(s32[2]{0:T(128)} %ro_ref.1, s32[2]{0:T(128)} %co_ref.1, s32[1,512]{1,0:T(1,128)} %bitcast.5, s32[1,512]{1,0:T(1,128)} %bitcast.6, s32[1,512]{1,0:T(1,128)} %bitcast.7, ...), custom_call_target="tpu_custom_call" | custom-call | tf_op jit(solution)/shard_map/cycle/pallas_call | solution.py:392
  45.3 0.0 copy-start
  45.3 5.0 %backward.1 = f32[512,512]{1,0:T(8,128)} custom-call(bf16[2,2,512,256]{3,2,1,0:T(8,128)(2,1)} %bitcast.4, bf16[512,1024]{1,0:T(8,128)(2,1)} %get-tuple-element.8.ar_ref, bf16[512,1024]{1,0:T(8,128)(2,1)} %get-tuple-element.9.ai_ref, bf16[2,512,512]{2,1,0:T(8,128)(2,1)} %get-tuple-element.10.bt_ref), custom_call_target="tpu_custom_call" | custom-call | tf_op jit(solution)/shard_map/backward/pallas_call | solution.py:465
  50.3 0.0 copy-done
  50.3 0.6 %copy.10 = f32[2,512]{1,0:T(2,128)} copy(f32[2,512]{1,0:T(2,128)S(1)} %copy-done) | data formatting | bytes 8192
Async XLA Ops:
  45.3 5.0 %copy-start = (f32[2,512]{1,0:T(2,128)S(1)}, f32[2,512]{1,0:T(2,128)}, u32[]{:S(2)}) copy-start(f32[2,512]{1,0:T(2,128)} %get-tuple-element.15) | copy-start | bytes 12292

commit v3 on v2

--- a/solution.py
+++ b/solution.py
@@ -144,63 +144,82 @@
 
     kcos = kk[...]
     ksin = ks[...]
-
-    def compose(n):
+    wide = SG // 2
+    waves = range(2)
+
+    def compose(n, start, unit):
+        places = (start + lax.broadcasted_iota(i32, (1, n), 1)) * unit
+        expand(0, places, rc.at[:, :n], rs.at[:, :n])
         c = rc[:, :n]
         s = rs[:, :n]
         re = jnp.dot(kcos, c, preferred_element_type=f32) + jnp.dot(ksin, s, preferred_element_type=f32)
         im = jnp.dot(ksin, c, preferred_element_type=f32) - jnp.dot(kcos, s, preferred_element_type=f32)
-        return re.astype(bf16), im.astype(bf16)
-
-    step = SKY // (cols * fs)
-    places = (lax.axis_index("fcol") * fs + lax.broadcasted_iota(i32, (1, fs), 1)) * step
+
+        def shifted(offset):
+            cos, sin = phase(offset * places)
+            return (re * cos + im * sin).astype(bf16), (im * cos - re * sin).astype(bf16)
+
+        return shifted
+
+    shifted = compose(fs, lax.axis_index("fcol") * fs, SKY // (cols * fs))
     for c in range(NC):
-        expand(co_ref[c], places, rc.at[:, :fs], rs.at[:, :fs])
-        re, im = compose(fs)
-        bt_ref[c, :SG] = re
-        bt_ref[c, SG:] = im
-    step = SKY // (rows * fs)
-    places = (x * (2 * fs) + lax.broadcasted_iota(i32, (1, 2 * fs), 1)) * step
+        bt_ref[c, :SG], bt_ref[c, SG:] = shifted(co_ref[c])
+    shifted = compose(2 * fs, x * (2 * fs), SKY // (rows * fs))
     for r in range(NR):
-        expand(ro_ref[r], places, rc, rs)
-        re, im = compose(2 * fs)
-        ar_ref[r * SG : r * SG + SG] = re
-        ai_ref[r * SG : r * SG + SG] = im
+        cut = slice(r * SG, r * SG + SG)
+        ar_ref[cut], ai_ref[cut] = shifted(ro_ref[r])
 
     mine.wait()
-    bt = bt_ref[h]
-
-    def project(ref):
-        return lax.dot_general(ref[...], bt, (((1,), (1,)), ((), ())), preferred_element_type=f32).astype(bf16)
-
-    own_p = project(facet_ref)
-    peers(lambda d, to, frm: link(d, to, frm).wait_recv())
-    k_vis = send(vis_all.at[h], vis_all.at[h], sib)
-    land(k_facet, other)
-    other_p = project(other)
+
+    def project(ref, w):
+        re = bt_ref[h, w * wide : (w + 1) * wide]
+        im = bt_ref[h, SG + w * wide : SG + (w + 1) * wide]
+        b = jnp.concatenate([re, im], 0)
+        return lax.dot_general(ref[...], b, (((1,), (1,)), ((), ())), preferred_element_type=f32).astype(bf16)
+
     part = NR * SG // (nx * ny)
     own_cut = pl.ds(pl.multiple_of(h * fs, fs), fs)
     other_cut = pl.ds(pl.multiple_of((1 - h) * fs, fs), fs)
-    first_a, first_b = [], []
-    for dx in list(range(1, nx)) + [0]:
-        px = lax.rem(x + dx, nx)
-        for dy in list(range(1, ny)) + [0]:
-            py = lax.rem(y + dy, ny)
-            cut = pl.ds(pl.multiple_of((px * ny + py) * part, part), part)
-            one = jnp.dot(ar_ref[cut, own_cut], own_p, preferred_element_type=f32)
-            one += jnp.dot(ar_ref[cut, other_cut], other_p, preferred_element_type=f32)
-            two = jnp.dot(ai_ref[cut, own_cut], own_p, preferred_element_type=f32)
-            two += jnp.dot(ai_ref[cut, other_cut], other_p, preferred_element_type=f32)
-            zr = one[:, :SG] - two[:, SG:]
-            zi = one[:, SG:] + two[:, :SG]
-            z_ref[0, px, py] = zr
-            z_ref[1, px, py] = zi
-            zb_ref[0, px, py] = zr.astype(bf16)
-            zb_ref[1, px, py] = zi.astype(bf16)
-            if dx == 0 and dy > 0:
-                first_b.append(send(zb_ref.at[1, :, py], got_b1.at[dy - 1], device((x * ny + py) * nz + z, h)))
-        if dx > 0:
-            first_a.append(send(zb_ref.at[0, px], got_a1.at[dx - 1], device((px * ny + y) * nz + z, h)))
+    first_a, first_b, second_a, second_b = [[], []], [[], []], [[], []], [[], []]
+    third, fourth, fifth_a, fifth_b = [[], []], [[], []], [[], []], [[], []]
+    sixth_a, sixth_b = [[], []], [[], []]
+
+    def to_x(d):
+        return device((lax.rem(x + d, nx) * ny + y) * nz + z, h)
+
+    def to_y(d):
+        return device((x * ny + lax.rem(y + d, ny)) * nz + z, h)
+
+    def to_z(d):
+        return device((x * ny + y) * nz + lax.rem(z + d, nz), h)
+
+    for w in waves:
+        own_p = project(facet_ref, w)
+        if w == 0:
+            land(k_facet, other)
+        other_p = project(other, w)
+        for dx in list(range(1, nx)) + [0]:
+            px = lax.rem(x + dx, nx)
+            for dy in list(range(1, ny)) + [0]:
+                py = lax.rem(y + dy, ny)
+                cut = pl.ds(pl.multiple_of((px * ny + py) * part, part), part)
+                one = jnp.dot(ar_ref[cut, own_cut], own_p, preferred_element_type=f32)
+                one += jnp.dot(ar_ref[cut, other_cut], other_p, preferred_element_type=f32)
+                two = jnp.dot(ai_ref[cut, own_cut], own_p, preferred_element_type=f32)
+                two += jnp.dot(ai_ref[cut, other_cut], other_p, preferred_element_type=f32)
+                zr = one[:, :wide] - two[:, wide:]
+                zi = one[:, wide:] + two[:, :wide]
+                z_ref[w, 0, px, py] = zr
+                z_ref[w, 1, px, py] = zi
+                zb_ref[w, 0, px, py] = zr.astype(bf16)
+                zb_ref[w, 1, px, py] = zi.astype(bf16)
+                if dx == 0 and dy > 0:
+                    first_b[w].append(send(zb_ref.at[w, 1, :, py], got_b1.at[w, dy - 1], to_y(dy)))
+            if dx > 0:
+                first_a[w].append(send(zb_ref.at[w, 0, px], got_a1.at[w, dx - 1], to_x(dx)))
+
+    peers(lambda d, to, frm: link(d, to, frm).wait_recv())
+    k_vis = send(vis_all.at[h], vis_all.at[h], sib)
 
     base = me * rows_own
     grid_acc[...] = jnp.zeros_like(grid_acc)
@@ -226,71 +245,114 @@
         lax.fori_loop(0, (hi - lo) // 2, body, 0)
 
     half = chips // 2
-    gridding(h, 0, half + half // 2)
-    for k, dst in zip(first_a, range(nx - 1)):
-        land(k, got_a1.at[dst])
-    total = z_ref[0, x]
-    for d in range(nx - 1):
-        total = total + got_a1[d].astype(f32)
-    acc_a[...] = total
-    send_a[...] = total.astype(bf16)
-    second_a, second_b = [], []
-    for d in range(1, ny):
-        py = lax.rem(y + d, ny)
-        second_a.append(send(send_a.at[py], got_a2.at[d - 1], device((x * ny + py) * nz + z, h)))
-    for k, dst in zip(first_b, range(ny - 1)):
-        land(k, got_b1.at[dst])
-    total = z_ref[1, :, y]
-    for d in range(ny - 1):
-        total = total + got_b1[d].astype(f32)
-    acc_b[...] = total
-    send_b[...] = total.astype(bf16)
-    for d in range(1, nx):
-        px = lax.rem(x + d, nx)
-        second_b.append(send(send_b.at[px], got_b2.at[d - 1], device((px * ny + y) * nz + z, h)))
-    gridding(h, half + half // 2, chips)
-    land(k_vis, vis_all.at[1 - h])
-    gridding(1 - h, 0, half // 2)
-    for k, dst in zip(second_a, range(ny - 1)):
-        land(k, got_a2.at[dst])
-    re = acc_a[y]
-    for d in range(ny - 1):
-        re = re + got_a2[d].astype(f32)
-    for k, dst in zip(second_b, range(nx - 1)):
-        land(k, got_b2.at[dst])
-    im = acc_b[x]
-    for d in range(nx - 1):
-        im = im + got_b2[d].astype(f32)
-    for k in range(nz):
-        cut = slice(k * rows_own, (k + 1) * rows_own)
-        own_z[k, :, :SG] = re[cut]
-        own_z[k, :, SG:] = im[cut]
-        send_z[k, :, :SG] = re[cut].astype(bf16)
-        send_z[k, :, SG:] = im[cut].astype(bf16)
-    third = []
-    for d in range(1, nz):
-        pz = lax.rem(z + d, nz)
-        third.append(send(send_z.at[pz], got_z.at[d - 1], device((x * ny + y) * nz + pz, h)))
-    gridding(1 - h, half // 2, chips)
-    for k, dst in zip(third, range(nz - 1)):
-        land(k, got_z.at[dst])
-    total = own_z[z]
-    for d in range(nz - 1):
-        total = total + got_z[d].astype(f32)
-    m = total * scale
-    got = [grid_acc[p * rows_own : (p + 1) * rows_own] for p in range(5)]
-    hat_re = got[0] + got[1] - got[4] * m[:, :SG]
-    hat_im = got[2] + got[3] - got[4] * m[:, SG:]
-    gz[z, :, :SG] = hat_re.astype(bf16)
-    gz[z, :, SG:] = hat_im.astype(bf16)
-    fourth = []
-    for d in range(1, nz):
-        pz = lax.rem(z + d, nz)
-        fourth.append(send(gz.at[z], gz.at[z], device((x * ny + y) * nz + pz, h)))
-    both = jnp.concatenate([m[:, :SG], m[:, SG:]], 0)
-    high = both.astype(bf16)
-    model[: 2 * rows_own] = high
-    model[2 * rows_own :] = (both - high.astype(f32)).astype(bf16)
+
+    def stage_two(w):
+        for d in range(nx - 1):
+            land(first_a[w][d], got_a1.at[w, d])
+        total = z_ref[w, 0, x]
+        for d in range(nx - 1):
+            total = total + got_a1[w, d].astype(f32)
+        acc_a[w] = total
+        send_a[w] = total.astype(bf16)
+        for d in range(1, ny):
+            second_a[w].append(send(send_a.at[w, lax.rem(y + d, ny)], got_a2.at[w, d - 1], to_y(d)))
+        for d in range(ny - 1):
+            land(first_b[w][d], got_b1.at[w, d])
+        total = z_ref[w, 1, :, y]
+        for d in range(ny - 1):
+            total = total + got_b1[w, d].astype(f32)
+        acc_b[w] = total
+        send_b[w] = total.astype(bf16)
+        for d in range(1, nx):
+            second_b[w].append(send(send_b.at[w, lax.rem(x + d, nx)], got_b2.at[w, d - 1], to_x(d)))
+
+    def stage_three(w):
+        for d in range(ny - 1):
+            land(second_a[w][d], got_a2.at[w, d])
+        re = acc_a[w, y]
+        for d in range(ny - 1):
+            re = re + got_a2[w, d].astype(f32)
+        for d in range(nx - 1):
+            land(second_b[w][d], got_b2.at[w, d])
+        im = acc_b[w, x]
+        for d in range(nx - 1):
+            im = im + got_b2[w, d].astype(f32)
+        for k in range(nz):
+            cut = slice(k * rows_own, (k + 1) * rows_own)
+            own_z[w, k, :, :wide] = re[cut]
+            own_z[w, k, :, wide:] = im[cut]
+            send_z[w, k, :, :wide] = re[cut].astype(bf16)
+            send_z[w, k, :, wide:] = im[cut].astype(bf16)
+        for d in range(1, nz):
+            third[w].append(send(send_z.at[w, lax.rem(z + d, nz)], got_z.at[w, d - 1], to_z(d)))
+
+    def turn(w):
+        for d in range(nz - 1):
+            land(third[w][d], got_z.at[w, d])
+        total = own_z[w, z]
+        for d in range(nz - 1):
+            total = total + got_z[w, d].astype(f32)
+        m = total * scale
+        cut = slice(w * wide, (w + 1) * wide)
+        got = [grid_acc[p * rows_own : (p + 1) * rows_own, cut] for p in range(5)]
+        hat_re = got[0] + got[1] - got[4] * m[:, :wide]
+        hat_im = got[2] + got[3] - got[4] * m[:, wide:]
+        gz[w, z, :, :wide] = hat_re.astype(bf16)
+        gz[w, z, :, wide:] = hat_im.astype(bf16)
+        for d in range(1, nz):
+            fourth[w].append(send(gz.at[w, z], gz.at[w, z], to_z(d)))
+        both = jnp.concatenate([m[:, :wide], m[:, wide:]], 0)
+        high = both.astype(bf16)
+        model[: 2 * rows_own, cut] = high
+        model[2 * rows_own :, cut] = (both - high.astype(f32)).astype(bf16)
+
+    cross = []
+
+    def over(index):
+        src = g_ref.at[(h,) + index]
+        cross.append((send(src, src, sib), index))
+
+    def stage_five(w):
+        for d in range(1, nz):
+            land(fourth[w][d - 1], gz.at[w, lax.rem(z - d + nz, nz)])
+        for k in range(nz):
+            cut = slice(k * rows_own, (k + 1) * rows_own)
+            g_ref[h, w, 0, x, y, cut, :] = gz[w, k, :, :wide]
+            g_ref[h, w, 1, x, y, cut, :] = gz[w, k, :, wide:]
+        for d in range(1, ny):
+            blk = g_ref.at[h, w, 0, x, y]
+            fifth_a[w].append(send(blk, blk, to_y(d)))
+        for d in range(1, nx):
+            blk = g_ref.at[h, w, 1, x, y]
+            fifth_b[w].append(send(blk, blk, to_x(d)))
+        over((w, 0, x, y))
+        over((w, 1, x, y))
+
+    def stage_six(w):
+        for d in range(1, ny):
+            land(fifth_a[w][d - 1], g_ref.at[h, w, 0, x, lax.rem(y - d + ny, ny)])
+        for d in range(1, nx):
+            blk = g_ref.at[h, w, 0, x]
+            sixth_a[w].append(send(blk, blk, to_x(d)))
+        for d in range(1, nx):
+            land(fifth_b[w][d - 1], g_ref.at[h, w, 1, lax.rem(x - d + nx, nx), y])
+        for d in range(1, ny):
+            blk = g_ref.at[h, w, 1, :, y]
+            sixth_b[w].append(send(blk, blk, to_y(d)))
+        for d in range(1, ny):
+            over((w, 0, x, lax.rem(y - d + ny, ny)))
+        for d in range(1, nx):
+            over((w, 1, lax.rem(x - d + nx, nx), y))
+
+    def finish(w):
+        for d in range(1, nx):
+            px = lax.rem(x - d + nx, nx)
+            land(sixth_a[w][d - 1], g_ref.at[h, w, 0, px])
+            over((w, 0, px))
+        for d in range(1, ny):
+            py = lax.rem(y - d + ny, ny)
+            land(sixth_b[w][d - 1], g_ref.at[h, w, 1, :, py])
+            over((w, 1, slice(None), py))
 
     def degrid(side, lo, hi):
         def one(q):
@@ -310,63 +372,37 @@
 
         lax.fori_loop(0, (hi - lo) // 2, body, 0)
 
-    degrid(1 - h, 0, chips)
-    k_vals = send(vals.at[1 - h], pair_vals, sib)
-    for k, d in zip(fourth, range(1, nz)):
-        land(k, gz.at[lax.rem(z - d + nz, nz)])
-    for k in range(nz):
-        cut = slice(k * rows_own, (k + 1) * rows_own)
-        g_ref[h, 0, x, y, cut, :] = gz[k, :, :SG]
-        g_ref[h, 1, x, y, cut, :] = gz[k, :, SG:]
-    fifth_a, fifth_b, cross = [], [], []
-
-    def over(index):
-        src = g_ref.at[(h,) + index]
-        cross.append((send(src, src, sib), index))
-
-    for d in range(1, ny):
-        blk = g_ref.at[h, 0, x, y]
-        fifth_a.append(send(blk, blk, device((x * ny + lax.rem(y + d, ny)) * nz + z, h)))
-    for d in range(1, nx):
-        blk = g_ref.at[h, 1, x, y]
-        fifth_b.append(send(blk, blk, device((lax.rem(x + d, nx) * ny + y) * nz + z, h)))
-    over((0, x, y))
-    over((1, x, y))
-    degrid(h, 0, half)
-    for k, d in zip(fifth_a, range(1, ny)):
-        land(k, g_ref.at[h, 0, x, lax.rem(y - d + ny, ny)])
-    sixth_a, sixth_b = [], []
-    for d in range(1, nx):
-        blk = g_ref.at[h, 0, x]
-        sixth_a.append(send(blk, blk, device((lax.rem(x + d, nx) * ny + y) * nz + z, h)))
-    for k, d in zip(fifth_b, range(1, nx)):
-        land(k, g_ref.at[h, 1, lax.rem(x - d + nx, nx), y])
-    for d in range(1, ny):
-        blk = g_ref.at[h, 1, :, y]
-        sixth_b.append(send(blk, blk, device((x * ny + lax.rem(y + d, ny)) * nz + z, h)))
-    for d in range(1, ny):
-        over((0, x, lax.rem(y - d + ny, ny)))
-    for d in range(1, nx):
-        over((1, lax.rem(x - d + nx, nx), y))
-    degrid(h, half, chips)
-    land(k_vals, pair_vals)
-    vals[h] = vals[h] + pair_vals[...]
-
     def back(d, to, slot):
         return pltpu.make_async_remote_copy(
             vals.at[h, to], slots.at[slot], ws.at[d], wr.at[d],
             device_id=device(to, h), device_id_type=MESH,
         )
 
+    stage_two(0)
+    gridding(h, 0, half)
+    stage_two(1)
+    gridding(h, half, chips)
+    stage_three(0)
+    land(k_vis, vis_all.at[1 - h])
+    gridding(1 - h, 0, half)
+    stage_three(1)
+    gridding(1 - h, half, chips)
+    turn(0)
+    turn(1)
+    degrid(1 - h, 0, half)
+    stage_five(0)
+    degrid(1 - h, half, chips)
+    k_vals = send(vals.at[1 - h], pair_vals, sib)
+    stage_five(1)
+    degrid(h, 0, half)
+    stage_six(0)
+    degrid(h, half, chips)
+    stage_six(1)
+    land(k_vals, pair_vals)
+    vals[h] = vals[h] + pair_vals[...]
     peers(lambda d, to, frm: back(d, to, me).start())
-    for k, d in zip(sixth_a, range(1, nx)):
-        px = lax.rem(x - d + nx, nx)
-        land(k, g_ref.at[h, 0, px])
-        over((0, px))
-    for k, d in zip(sixth_b, range(1, ny)):
-        py = lax.rem(y - d + ny, ny)
-        land(k, g_ref.at[h, 1, :, py])
-        over((1, slice(None), py))
+    finish(0)
+    finish(1)
     peers(lambda d, to, frm: back(d, to, frm).wait_recv())
     start = vals[h, me]
     res_ref[...] = obs_ref[...] - lax.fori_loop(
@@ -387,12 +423,12 @@
     nv = obs.shape[1]
     rows_own = NR * SG // chips
     long = nz * rows_own
-    copies = 64
+    copies = 128
     dma = pltpu.SemaphoreType.DMA
     return pl.pallas_call(
         functools.partial(main_kernel, scale),
         out_shape=[
-            jax.ShapeDtypeStruct((2, 2, nx, ny, long, SG), bf16),
+            jax.ShapeDtypeStruct((2, 2, 2, nx, ny, long, SG // 2), bf16),
             jax.ShapeDtypeStruct((NR * SG, 2 * fs), bf16),
             jax.ShapeDtypeStruct((NR * SG, 2 * fs), bf16),
             jax.ShapeDtypeStruct((NC, 2 * SG, fs), bf16),
@@ -408,21 +444,21 @@
             pltpu.VMEM((4, nv), f32),
             pltpu.VMEM((2, chips, 4, nv), f32),
             pltpu.VMEM((fs, fs), bf16),
-            pltpu.VMEM((2, nx, ny, long, SG), f32),
-            pltpu.VMEM((2, nx, ny, long, SG), bf16),
+            pltpu.VMEM((2, 2, nx, ny, long, SG // 2), f32),
+            pltpu.VMEM((2, 2, nx, ny, long, SG // 2), bf16),
             pltpu.VMEM((5 * rows_own, SG), f32),
-            pltpu.VMEM((ny, long, SG), f32),
-            pltpu.VMEM((nx, long, SG), f32),
-            pltpu.VMEM((ny, long, SG), bf16),
-            pltpu.VMEM((nx, long, SG), bf16),
-            pltpu.VMEM((nx - 1, ny, long, SG), bf16),
-            pltpu.VMEM((ny - 1, nx, long, SG), bf16),
-            pltpu.VMEM((ny - 1, long, SG), bf16),
-            pltpu.VMEM((nx - 1, long, SG), bf16),
-            pltpu.VMEM((nz, rows_own, 2 * SG), f32),
-            pltpu.VMEM((nz, rows_own, 2 * SG), bf16),
-            pltpu.VMEM((nz - 1, rows_own, 2 * SG), bf16),
-            pltpu.VMEM((nz, rows_own, 2 * SG), bf16),
+            pltpu.VMEM((2, ny, long, SG // 2), f32),
+            pltpu.VMEM((2, nx, long, SG // 2), f32),
+            pltpu.VMEM((2, ny, long, SG // 2), bf16),
+            pltpu.VMEM((2, nx, long, SG // 2), bf16),
+            pltpu.VMEM((2, nx - 1, ny, long, SG // 2), bf16),
+            pltpu.VMEM((2, ny - 1, nx, long, SG // 2), bf16),
+            pltpu.VMEM((2, ny - 1, long, SG // 2), bf16),
+            pltpu.VMEM((2, nx - 1, long, SG // 2), bf16),
+            pltpu.VMEM((2, nz, rows_own, SG), f32),
+            pltpu.VMEM((2, nz, rows_own, SG), bf16),
+            pltpu.VMEM((2, nz - 1, rows_own, SG), bf16),
+            pltpu.VMEM((2, nz, rows_own, SG), bf16),
             pltpu.VMEM((4 * rows_own, SG), bf16),
             pltpu.VMEM((2, chips, 2, nv), f32),
             pltpu.VMEM((chips, 2, nv), f32),
@@ -447,7 +483,7 @@
     fs = image_ref.shape[0]
     cut = pl.ds(pl.multiple_of(h * fs, fs), fs)
     first = (((0,), (0,)), ((), ()))
-    g = jnp.concatenate([g_ref[c, p] for c in range(NC) for p in range(2)], 1)
+    g = jnp.concatenate([g_ref[c, w, p] for c in range(NC) for p in range(2) for w in range(2)], 1)
     one = lax.dot_general(ar_ref[:, cut], g, first, preferred_element_type=f32)
     two = lax.dot_general(ai_ref[:, cut], g, first, preferred_element_type=f32)
     parts = []
@@ -481,7 +517,7 @@
         row_offsets, col_offsets, vis_subgrid[None], vis_u[None], vis_v[None],
         observed, facet_image, scale_in / SG,
     )
-    image = backward(g.reshape(NC, 2, NR * SG, SG), ar, ai, bt, scale_out / SG)
+    image = backward(g.reshape(NC, 2, 2, NR * SG, SG // 2), ar, ai, bt, scale_out / SG)
     return (image, residual)
 
 

time: 51.1 us -> 47.9 us (0.937)
  Pallas kernels: 49.7 us -> 46.5 us
    pallas_call x1, Pallas kernels: 44.7 us -> 41.5 us  [main(): pl.pallas_call(functools.partial(main_kernel, scale), out_shape=[jax.Shap...]
where the time goes in v3:
time: 47.9 us; the launch traced here: 47.7 us
  Pallas kernels  46.5 us (97%)
  between operations  0.65 us (1%)
  local copies, waits for them, and re-layouts  0.6 us (1%)
    pallas_call x1, Pallas kernels, main(): pl.pallas_call(functools.partial(main_kernel, scale), out_shape=[jax.Shap...  41.5 us
    pallas_call x1, Pallas kernels, backward(): pl.pallas_call(functools.partial(backward_kernel, scale), out_shape=jax.S...  4.99 us

profile of v3, /device:TPU:0, one launch (start us, length us, event | category | flops | bytes accessed | tf_op | source)
XLA Modules:
  0.0 47.7 jit_solution(6013807825576754515)
XLA Ops:
  0.6 41.5 %cycle.1 = (bf16[2,2,2,2,2,128,128]{6,5,4,3,2,1,0:T(8,128)(2,1)}, bf16[512,1024]{1,0:T(8,128)(2,1)}, bf16[512,1024]{1,0:T(8,128)(2,1)}, bf16[2,512,512]{2,1,0:T(8,128)(2,1)}, f32[2,512]{1,0:T(2,128)}) custom-call(s32[2]{0:T(128)} %ro_ref.1, s32[2]{0:T(128)} %co_ref.1, s32[1,512]{1,0:T(1,128)} %bitcast.5, s32[1,512]{1,0:T(1,128)} %bitcast.6, ...), custom_call_target="tpu_custom_call" | custom-call | tf_op jit(solution)/shard_map/cycle/pallas_call | solution.py:428
  42.1 0.0 copy-start
  42.1 5.0 %backward.1 = f32[512,512]{1,0:T(8,128)} custom-call(bf16[2,2,2,512,128]{4,3,2,1,0:T(8,128)(2,1)} %bitcast.4, bf16[512,1024]{1,0:T(8,128)(2,1)} %get-tuple-element.8.ar_ref, bf16[512,1024]{1,0:T(8,128)(2,1)} %get-tuple-element.9.ai_ref, bf16[2,512,512]{2,1,0:T(8,128)(2,1)} %get-tuple-element.10.bt_ref), custom_call_target="tpu_custom_call" | custom-call | tf_op jit(solution)/shard_map/backward/pallas_call | solution.py:501
  47.1 0.0 copy-done
  47.1 0.6 %copy.10 = f32[2,512]{1,0:T(2,128)} copy(f32[2,512]{1,0:T(2,128)S(1)} %copy-done) | data formatting | bytes 8192
Async XLA Ops:
  42.1 5.0 %copy-start = (f32[2,512]{1,0:T(2,128)S(1)}, f32[2,512]{1,0:T(2,128)}, u32[]{:S(2)}) copy-start(f32[2,512]{1,0:T(2,128)} %get-tuple-element.15) | copy-start | bytes 12292

commit v4 on v3

--- a/solution.py
+++ b/solution.py
@@ -114,7 +114,6 @@
     mine = pltpu.make_async_copy(vis_ref, vis_all.at[h, me], lsem)
     mine.start()
     expand(0, lax.broadcasted_iota(i32, (1, SG), 1) * (SKY // SG), kk, ks)
-    pl.semaphore_wait(barrier, chips)
     used = [0]
     sent = []
 
@@ -139,8 +138,6 @@
             device_id=device(to, h), device_id_type=MESH,
         )
 
-    k_facet = send(facet_ref, other, sib)
-    peers(lambda d, to, frm: link(d, to, me).start())
 
     kcos = kk[...]
     ksin = ks[...]
@@ -164,6 +161,9 @@
     shifted = compose(fs, lax.axis_index("fcol") * fs, SKY // (cols * fs))
     for c in range(NC):
         bt_ref[c, :SG], bt_ref[c, SG:] = shifted(co_ref[c])
+    pl.semaphore_wait(barrier, chips)
+    k_facet = send(facet_ref, other, sib)
+    peers(lambda d, to, frm: link(d, to, me).start())
     shifted = compose(2 * fs, x * (2 * fs), SKY // (rows * fs))
     for r in range(NR):
         cut = slice(r * SG, r * SG + SG)

time: 47.9 us -> 47 us (0.981)
  Pallas kernels: 46.5 us -> 45.6 us
    pallas_call x1, Pallas kernels: 41.5 us -> 40.6 us  [main(): pl.pallas_call(functools.partial(main_kernel, scale), out_shape=[jax.Shap...]
where the time goes in v4:
time: 47 us; the launch traced here: 46.9 us
  Pallas kernels  45.6 us (97%)
  between operations  0.65 us (1%)
  local copies, waits for them, and re-layouts  0.6 us (1%)
    pallas_call x1, Pallas kernels, main(): pl.pallas_call(functools.partial(main_kernel, scale), out_shape=[jax.Shap...  40.6 us
    pallas_call x1, Pallas kernels, backward(): pl.pallas_call(functools.partial(backward_kernel, scale), out_shape=jax.S...  4.99 us

profile of v4, /device:TPU:0, one launch (start us, length us, event | category | flops | bytes accessed | tf_op | source)
XLA Modules:
  0.0 46.9 jit_solution(14337284443446923350)
XLA Ops:
  0.6 40.6 %cycle.1 = (bf16[2,2,2,2,2,128,128]{6,5,4,3,2,1,0:T(8,128)(2,1)}, bf16[512,1024]{1,0:T(8,128)(2,1)}, bf16[512,1024]{1,0:T(8,128)(2,1)}, bf16[2,512,512]{2,1,0:T(8,128)(2,1)}, f32[2,512]{1,0:T(2,128)}) custom-call(s32[2]{0:T(128)} %ro_ref.1, s32[2]{0:T(128)} %co_ref.1, s32[1,512]{1,0:T(1,128)} %bitcast.5, s32[1,512]{1,0:T(1,128)} %bitcast.6, ...), custom_call_target="tpu_custom_call" | custom-call | tf_op jit(solution)/shard_map/cycle/pallas_call | solution.py:428
  41.3 0.0 copy-start
  41.3 5.0 %backward.1 = f32[512,512]{1,0:T(8,128)} custom-call(bf16[2,2,2,512,128]{4,3,2,1,0:T(8,128)(2,1)} %bitcast.4, bf16[512,1024]{1,0:T(8,128)(2,1)} %get-tuple-element.8.ar_ref, bf16[512,1024]{1,0:T(8,128)(2,1)} %get-tuple-element.9.ai_ref, bf16[2,512,512]{2,1,0:T(8,128)(2,1)} %get-tuple-element.10.bt_ref), custom_call_target="tpu_custom_call" | custom-call | tf_op jit(solution)/shard_map/backward/pallas_call | solution.py:501
  46.3 0.0 copy-done
  46.3 0.6 %copy.10 = f32[2,512]{1,0:T(2,128)} copy(f32[2,512]{1,0:T(2,128)S(1)} %copy-done) | data formatting | bytes 8192
Async XLA Ops:
  41.3 5.0 %copy-start = (f32[2,512]{1,0:T(2,128)S(1)}, f32[2,512]{1,0:T(2,128)}, u32[]{:S(2)}) copy-start(f32[2,512]{1,0:T(2,128)} %get-tuple-element.15) | copy-start | bytes 12292
